TPU v7x, 32 devices: a whole 2x2x4 slice. The times are simulated.
32 devices in a mesh: lat: 4 (over z), lon: 8 (over y, x, core).
Axes of the slice: x: 2, y: 2, z: 4, core: 2. Of those that a mesh axis runs over, the one named last changes fastest.
Arguments:
- grid_feats: float32 [4, 16, 128, 1024], P('lat', 'lon'), may hold values from -6 to 6
- lift_index: int32 [4, 24, 4], P('lat', 'lon'), may hold values from 0 to 63, as said below
- lift_weight: float32 [4, 24, 4, 128, 128], P('lat', 'lon'), may hold values from -0.25 to 0.25
- window_index: int32 [4, 24, 8], P('lat', 'lon'), may hold values from 0 to 95, as said below
- window_count: int32 [4, 24], P('lat', 'lon'), may hold values from 4 to 8
- norm_gains: float32 [2, 1024], replicated, may hold values from 0.5 to 1.5
- qkv_weight: bfloat16 [1024, 3072], replicated, may hold values from -6.5 to 6.5
- out_weight: bfloat16 [1024, 1024], replicated, may hold values from -0.1875 to 0.1875
- up_weight: bfloat16 [1024, 2048], replicated, may hold values from -0.1875 to 0.1875
- down_weight: bfloat16 [2048, 1024], replicated, may hold values from -0.125 to 0.125
- return_index: int32 [4, 16, 4], P('lat', 'lon'), may hold values from 0 to 95, as said below
- return_weight: float32 [4, 16, 4, 128, 128], P('lat', 'lon'), may hold values from -0.25 to 0.25
Outputs:
- grid_out: float32 [4, 16, 128, 1024], P('lat', 'lon')
Inputs may be any that keep to these rules, and one draw needn't show every extreme that they name: `lift_index`: entries name grid blocks a' * 16 + b'; the 4 entries of a row differ; for mesh block (a, c), |a' - a| <= 1 and b' lies among the 4 columns from c // 3 * 2 - 1 to c // 3 * 2 + 2, counted modulo 16. `window_index`: entries name mesh blocks a' * 24 + c'; slot 0 is the query block itself, the 8 entries of a row differ; |a' - a| <= 1 and c' lies among the 5 columns from c // 3 * 3 - 1 to c // 3 * 3 + 3, counted modulo 24. `return_index`: entries name mesh blocks a' * 24 + c'; the 4 entries of a row differ; for grid block (a, b), |a' - a| <= 1 and c' lies among the 5 columns from b // 2 * 3 - 1 to b // 2 * 3 + 3, counted modulo 24.
All inputs are finite; a program needn't handle non-finite values.
Results may differ from a plain program's by a relative error of at most 0.0035.
Values may be sent and summed in bfloat16 or wider, within the bound.
A program may use at most 128 MiB of HBM per device.

v0:
```python
import jax
import jax.numpy as jnp
from jax import lax
from jax.sharding import PartitionSpec as P

HEADS = 16


EPSILON = 1e-05


def with_halo(cells, sides, width):
    for axis, dim in sides:
        count = lax.axis_size(axis)
        head = lax.slice_in_dim(cells, 0, width, axis=dim)
        tail = lax.slice_in_dim(cells, cells.shape[dim] - width, cells.shape[dim], axis=dim)
        cells = jnp.concatenate(
            [
                lax.ppermute(tail, axis, [(i, (i + 1) % count) for i in range(count)]),
                cells,
                lax.ppermute(head, axis, [((i + 1) % count, i) for i in range(count)]),
            ],
            axis=dim,
        )
    return cells


def layer_norm(values, gain):
    centred = values - jnp.mean(values, axis=-1, keepdims=True)
    spread = jnp.mean(centred * centred, axis=-1, keepdims=True)
    return (centred * lax.rsqrt(spread + EPSILON) * gain).astype(jnp.bfloat16)


def gelu_exact(values):
    return 0.5 * values * (1.0 + lax.erf(values * 0.7071067811865476))


def local_slots(global_ids, total_lon, band_here, sector_here, blocks_here):
    source_band = global_ids // total_lon
    source_column = global_ids % total_lon
    band_offset = source_band - band_here + 1
    column_offset = (source_column - sector_here * blocks_here + 1) % total_lon
    return band_offset * (blocks_here + 2) + column_offset


def shards(
    grid_feats,
    lift_index,
    lift_weight,
    window_index,
    window_count,
    norm_gains,
    qkv_weight,
    out_weight,
    up_weight,
    down_weight,
    return_index,
    return_weight,
):
    lon_count = lax.axis_size("lon")
    band_here = lax.axis_index("lat")
    sector_here = lax.axis_index("lon")
    grid_blocks = grid_feats.shape[1]
    mesh_blocks = lift_index.shape[1]
    block_rows = grid_feats.shape[2]
    feature_width = grid_feats.shape[3]
    head_size = feature_width // HEADS
    grid_lon = grid_blocks * lon_count
    mesh_lon = mesh_blocks * lon_count
    padded_grid = with_halo(grid_feats, (("lat", 0), ("lon", 1)), 1)
    grid_table = padded_grid.reshape(-1, block_rows, feature_width)
    lift_slots = local_slots(lift_index[0], grid_lon, band_here, sector_here, grid_blocks)
    mesh_in = jnp.einsum(
        "mkrs,mksc->mrc", lift_weight[0], grid_table[lift_slots], precision=lax.Precision.HIGHEST
    )
    normed = layer_norm(mesh_in, norm_gains[0])
    flat_normed = normed.reshape(-1, feature_width)
    queries = jnp.dot(
        flat_normed, qkv_weight[:, :feature_width], preferred_element_type=jnp.float32
    ).astype(jnp.bfloat16)
    padded_normed = with_halo(
        normed.reshape(1, mesh_blocks, block_rows, feature_width), (("lat", 0), ("lon", 1)), 1
    )
    key_value = jnp.dot(
        padded_normed.reshape(-1, feature_width),
        qkv_weight[:, feature_width:],
        preferred_element_type=jnp.float32,
    ).astype(jnp.bfloat16)
    key_table = key_value.reshape(-1, block_rows, 2 * feature_width)
    window_slots = local_slots(window_index[0], mesh_lon, band_here, sector_here, mesh_blocks)
    neighbours = window_slots.shape[1]
    gathered = key_table[window_slots]
    keys = gathered[..., :feature_width].reshape(
        mesh_blocks, neighbours * block_rows, HEADS, head_size
    )
    values = gathered[..., feature_width:].reshape(
        mesh_blocks, neighbours * block_rows, HEADS, head_size
    )
    query_heads = queries.reshape(mesh_blocks, block_rows, HEADS, head_size)
    scores = jnp.einsum(
        "mqhd,mkhd->mhqk", query_heads, keys, preferred_element_type=jnp.float32
    ) * head_size ** (-0.5)
    key_block = jnp.arange(neighbours * block_rows, dtype=jnp.int32) // block_rows
    live = key_block[None, :] < window_count[0][:, None]
    masked = jnp.where(live[:, None, None, :], scores, -1e30)
    highest = jnp.max(masked, axis=-1, keepdims=True)
    raw_weights = jnp.exp(masked - highest)
    weights = (raw_weights / jnp.sum(raw_weights, axis=-1, keepdims=True)).astype(jnp.bfloat16)
    mixed = jnp.einsum("mhqk,mkhd->mqhd", weights, values, preferred_element_type=jnp.float32)
    mixed = mixed.astype(jnp.bfloat16).reshape(-1, feature_width)
    after_attention = mesh_in.reshape(-1, feature_width) + jnp.dot(
        mixed, out_weight, preferred_element_type=jnp.float32
    )
    normed_again = layer_norm(after_attention, norm_gains[1])
    hidden_units = gelu_exact(
        jnp.dot(normed_again, up_weight, preferred_element_type=jnp.float32)
    ).astype(jnp.bfloat16)
    mesh_out = after_attention + jnp.dot(
        hidden_units, down_weight, preferred_element_type=jnp.float32
    )
    padded_mesh = with_halo(
        mesh_out.reshape(1, mesh_blocks, block_rows, feature_width), (("lat", 0), ("lon", 1)), 1
    )
    mesh_table = padded_mesh.reshape(-1, block_rows, feature_width)
    return_slots = local_slots(return_index[0], mesh_lon, band_here, sector_here, mesh_blocks)
    grid_out = jnp.einsum(
        "gkrs,gksc->grc",
        return_weight[0],
        mesh_table[return_slots],
        precision=lax.Precision.HIGHEST,
    )
    return grid_out.reshape(1, grid_blocks, block_rows, feature_width)


def solution(mesh):
    placed = (
        P("lat", "lon", None, None),
        P("lat", "lon", None),
        P("lat", "lon", None, None, None),
        P("lat", "lon", None),
        P("lat", "lon"),
        P(),
        P(),
        P(),
        P(),
        P(),
        P("lat", "lon", None),
        P("lat", "lon", None, None, None),
    )
    return jax.shard_map(
        shards, mesh=mesh, in_specs=placed, out_specs=P("lat", "lon", None, None), check_vma=False
    )
```

profile of v0, /device:TPU:0, one launch (start us, length us, event | category | flops | bytes accessed | tf_op | source)
XLA Modules:
  0.0 418.5 jit_solution(15880568074674783404)
XLA Ops:
  5.1 24.2 %collective-permute-done = f32[1,2,128,1024]{3,2,1,0:T(8,128)S(1)} collective-permute-done((f32[1,2,128,1024]{3,2,1,0:T(8,128)}, f32[1,2,128,1024]{3,2,1,0:T(8,128)S(1)}, u32[]{:S(2)}, u32[]{:S(2)}) %collective-permute-start) | collective-permute-done | bytes 1048608 | tf_op jit(solution)/shard_map/ppermute | solution.py:19
  30.7 19.6 %collective-permute-done.1 = f32[1,2,128,1024]{3,2,1,0:T(8,128)S(1)} collective-permute-done((f32[1,2,128,1024]{3,2,1,0:T(8,128)}, f32[1,2,128,1024]{3,2,1,0:T(8,128)S(1)}, u32[]{:S(2)}, u32[]{:S(2)}) %collective-permute-start.1) | collective-permute-done | bytes 1048608 | tf_op jit(solution)/shard_map/ppermute | solution.py:21
  54.8 34.4 %collective-permute-done.3 = f32[3,1,128,1024]{3,2,1,0:T(8,128)} collective-permute-done((f32[3,1,128,1024]{3,2,1,0:T(8,128)}, f32[3,1,128,1024]{3,2,1,0:T(8,128)}, u32[]{:S(2)}, u32[]{:S(2)}) %collective-permute-start.3) | collective-permute-done | bytes 1572896 | tf_op jit(solution)/shard_map/ppermute | solution.py:21
  91.1 6.6 %pad_maximum_fusion.1 = f32[3,4,128,1024]{3,2,1,0:T(8,128)} fusion(f32[3,1,128,1024]{3,2,1,0:T(8,128)} %collective-permute-done.3, f32[3,2,128,1024]{3,2,1,0:T(8,128)} %copy-done.4, f32[3,1,128,1024]{3,2,1,0:T(8,128)} %collective-permute-done.2), kind=kLoop, calls=%fused_computation.14 | loop fusion | flops 3145728 | bytes 12582912 | tf_op jit(solution)/shard_map/concatenate | solution.py:17
  97.7 6.5 %gather_fusion = f32[12,128,1024]{2,1,0:T(8,128)} fusion(f32[12,128,1024]{2,1,0:T(8,128)} %bitcast.134, s32[1024]{0:T(1024)S(1)} %pad_clamp_fusion.2), kind=kCustom, calls=%fused_computation | custom fusion | bytes 12582960 | tf_op jit(solution)/shard_map/gather | solution.py:74
  104.2 6.0 %bitcast_reduce_fusion = (f32[3,128]{1,0:T(4,128)S(1)}, f32[3,1024,128,1]{1,2,3,0:T(8,128)S(1)}) fusion(f32[3,4,128,1024]{3,2,1,0:T(8,128)} %bitcast.135, f32[1,3,4,128,128]{4,3,2,1,0:T(8,128)S(1)} %copy-done.8), kind=kOutput, calls=%fused_computation.25 | convolution fusion | flops 2416311808 | bytes 8652288 | tf_op jit(solution)/shard_map/mkrs,mksc->mrc/dot_general | solution.py:73
  115.3 17.8 %collective-permute-done.5 = bf16[1,3,128,1024]{3,2,1,0:T(8,128)(2,1)} collective-permute-done((bf16[1,3,128,1024]{3,2,1,0:T(8,128)(2,1)S(1)}, bf16[1,3,128,1024]{3,2,1,0:T(8,128)(2,1)}, u32[]{:S(2)}, u32[]{:S(2)}) %collective-permute-start.5) | collective-permute-done | bytes 786464 | tf_op jit(solution)/shard_map/ppermute | solution.py:21
  133.1 15.3 %collective-permute-done.4 = bf16[1,3,128,1024]{3,2,1,0:T(8,128)(2,1)} collective-permute-done((bf16[1,3,128,1024]{3,2,1,0:T(8,128)(2,1)S(1)}, bf16[1,3,128,1024]{3,2,1,0:T(8,128)(2,1)}, u32[]{:S(2)}, u32[]{:S(2)}) %collective-permute-start.4) | collective-permute-done | bytes 786464 | tf_op jit(solution)/shard_map/ppermute | solution.py:19
  158.4 10.1 %collective-permute-done.7 = bf16[3,1,128,1024]{3,2,1,0:T(8,128)(2,1)} collective-permute-done((bf16[3,1,128,1024]{3,2,1,0:T(8,128)(2,1)}, bf16[3,1,128,1024]{3,2,1,0:T(8,128)(2,1)}, u32[]{:S(2)}, u32[]{:S(2)}) %collective-permute-start.7) | collective-permute-done | bytes 786464 | tf_op jit(solution)/shard_map/ppermute | solution.py:21
  173.8 12.4 %convolution_convert_fusion = bf16[1920,2048]{1,0:T(8,128)(2,1)} fusion(bf16[1920,1024]{1,0:T(8,128)(2,1)S(1)} %bitcast.143, bf16[1024,3072]{1,0:T(8,128)(2,1)} %param.18), kind=kOutput, calls=%fused_computation.13 | convolution fusion | flops 8056995840 | bytes 15990784 | tf_op jit(solution)/shard_map/dot_general | solution.py:84
  186.2 9.3 %gather_fusion.1 = bf16[24,128,2048]{2,1,0:T(8,128)(2,1)} fusion(bf16[15,128,2048]{2,1,0:T(8,128)(2,1)} %bitcast.136, s32[1024]{0:T(1024)S(1)} %pad_clamp_fusion.1), kind=kCustom, calls=%fused_computation.1 | custom fusion | bytes 25165920 | tf_op jit(solution)/shard_map/gather | solution.py:92
  195.5 10.7 %fusion.64 = (bf16[3,8,128,1024]{3,2,1,0:T(8,128)(2,1)}, bf16[3,8,128,1024]{3,2,1,0:T(8,128)(2,1)}) fusion(bf16[3,8,128,2048]{3,2,1,0:T(8,128)(2,1)} %bitcast.133), kind=kLoop, calls=%fused_computation.119 | loop fusion | bytes 25165824 | tf_op jit(solution)/shard_map/slice | solution.py:93
  206.1 9.0 %copy.42 = bf16[3,8,128,1024]{2,1,3,0:T(8,128)(2,1)} copy(bf16[3,8,128,1024]{3,2,1,0:T(8,128)(2,1)} %get-tuple-element.6) | data formatting | bytes 12582912
  215.1 10.3 %reshape.479 = bf16[3,1024,16,64]{1,3,2,0:T(8,128)(2,1)} reshape(bf16[3,8,128,1024]{2,1,3,0:T(8,128)(2,1)} %copy.42) | data formatting | bytes 12582912 | tf_op jit(solution)/shard_map/reshape | solution.py:96
  225.4 9.0 %copy.43 = bf16[3,8,128,1024]{2,1,3,0:T(8,128)(2,1)} copy(bf16[3,8,128,1024]{3,2,1,0:T(8,128)(2,1)} %get-tuple-element.5) | data formatting | bytes 12582912
  234.4 10.3 %reshape.482 = bf16[3,1024,16,64]{1,3,2,0:T(8,128)(2,1)} reshape(bf16[3,8,128,1024]{2,1,3,0:T(8,128)(2,1)} %copy.43) | data formatting | bytes 12582912 | tf_op jit(solution)/shard_map/reshape | solution.py:93
  244.7 15.3 %fusion.67 = (f32[3,16,128]{2,1,0:T(8,128)S(1)}, f32[3,16,128,1024]{3,2,1,0:T(8,128)}) fusion(pred[3,1024]{1,0:T(4,128)(4,1)S(1)} %broadcast_compare_fusion, bf16[3,1024,16,64]{1,3,2,0:T(8,128)(2,1)} %reshape.482, bf16[3,128,16,64]{3,2,1,0:T(8,128)(2,1)} %reshape.516), kind=kOutput, calls=%fused_computation.122 | convolution fusion | flops 830473216 | bytes 32271360 | tf_op jit(solution)/shard_map/sub | solution.py:107
  259.9 12.7 %fusion.24 = bf16[3,128,16,64]{1,3,2,0:T(8,128)(2,1)S(1)} fusion(bf16[3,1024,16,64]{1,3,2,0:T(8,128)(2,1)} %reshape.479, f32[3,16,128,1024]{3,2,1,0:T(8,128)} %get-tuple-element.20, f32[3,16,128]{2,1,0:T(8,128)S(1)} %get-tuple-element.19), kind=kOutput, calls=%fused_computation.39 | convolution fusion | flops 818282496 | bytes 32268288 | tf_op jit(solution)/shard_map/mhqk,mkhd->mqhd/dot_general | solution.py:109
  276.0 9.2 %fusion.12 = f32[384,1024]{1,0:T(8,128)} fusion(f32[384,1024]{1,0:T(8,128)} %copy-done.5, bf16[2048,1024]{1,0:T(8,128)(2,1)} %param.21, bf16[1024,2048]{1,0:T(8,128)(2,1)} %param.20, f32[1024]{0:T(1024)S(1)} %bitcast.148, f32[384]{0:T(512)S(1)} %add_rsqrt_fusion, f32[384]{0:T(512)S(1)} %broadcast_multiply_fusion), kind=kOutput, calls=%fused_computation.32 | convolution fusion | flops 3227123712 | bytes 11541504 | tf_op jit(solution)/shard_map/dot_general | solution.py:118
  287.2 35.1 %collective-permute-done.9 = f32[1,3,128,1024]{3,2,1,0:T(8,128)S(1)} collective-permute-done((f32[1,3,128,1024]{3,2,1,0:T(8,128)}, f32[1,3,128,1024]{3,2,1,0:T(8,128)S(1)}, u32[]{:S(2)}, u32[]{:S(2)}) %collective-permute-start.9) | collective-permute-done | bytes 1572896 | tf_op jit(solution)/shard_map/ppermute | solution.py:21
  322.3 31.5 %collective-permute-done.8 = f32[1,3,128,1024]{3,2,1,0:T(8,128)S(1)} collective-permute-done((f32[1,3,128,1024]{3,2,1,0:T(8,128)}, f32[1,3,128,1024]{3,2,1,0:T(8,128)S(1)}, u32[]{:S(2)}, u32[]{:S(2)}) %collective-permute-start.8) | collective-permute-done | bytes 1572896 | tf_op jit(solution)/shard_map/ppermute | solution.py:19
  360.5 34.7 %collective-permute-done.11 = f32[3,1,128,1024]{3,2,1,0:T(8,128)} collective-permute-done((f32[3,1,128,1024]{3,2,1,0:T(8,128)}, f32[3,1,128,1024]{3,2,1,0:T(8,128)}, u32[]{:S(2)}, u32[]{:S(2)}) %collective-permute-start.11) | collective-permute-done | bytes 1572896 | tf_op jit(solution)/shard_map/ppermute | solution.py:21
  402.5 6.0 %gather_fusion.2 = f32[8,128,1024]{2,1,0:T(8,128)} fusion(f32[15,128,1024]{2,1,0:T(8,128)} %bitcast.137, s32[1024]{0:T(1024)S(1)} %pad_clamp_fusion), kind=kCustom, calls=%fused_computation.2 | custom fusion | bytes 8388640 | tf_op jit(solution)/shard_map/gather | solution.py:129
  408.5 8.6 %convolution_bitcast_fusion = f32[1,2,128,1024]{2,3,1,0:T(8,128)S(1)} fusion(f32[2,4,128,1024]{3,2,1,0:T(8,128)} %bitcast.138, f32[1,2,4,128,128]{4,3,2,1,0:T(8,128)} %param.23), kind=kOutput, calls=%fused_computation.38 | convolution fusion | flops 1610612736 | bytes 5767168 | tf_op jit(solution)/shard_map/gkrs,gksc->grc/dot_general | solution.py:126
  (78 shorter events, 53.8 us)
Async XLA Ops:
  0.0 273.4 %copy-start = (bf16[1024,1024]{1,0:T(8,128)(2,1)S(1)}, bf16[1024,1024]{1,0:T(8,128)(2,1)}, u32[]{:S(2)}) copy-start(bf16[1024,1024]{1,0:T(8,128)(2,1)} %param.19) | copy-start | bytes 6291460
  0.0 29.3 %collective-permute-start = (f32[1,2,128,1024]{3,2,1,0:T(8,128)}, f32[1,2,128,1024]{3,2,1,0:T(8,128)S(1)}, u32[]{:S(2)}, u32[]{:S(2)}) collective-permute-start(f32[1,2,128,1024]{3,2,1,0:T(8,128)} %param.12), channel_id=1, source_target_pairs={{0,8},{8,16},{16,24},{24,0},{1,9},{9,17},{17,25},{25,1},{2,10},{10... | collective-permute-start | bytes 3145736 | tf_op jit(solution)/shard_map/ppermute | solution.py:19
  3.1 47.3 %collective-permute-start.1 = (f32[1,2,128,1024]{3,2,1,0:T(8,128)}, f32[1,2,128,1024]{3,2,1,0:T(8,128)S(1)}, u32[]{:S(2)}, u32[]{:S(2)}) collective-permute-start(f32[1,2,128,1024]{3,2,1,0:T(8,128)} %param.12), channel_id=1, source_target_pairs={{8,0},{16,8},{24,16},{0,24},{9,1},{17,9},{25,17},{1,25},{10,2},{18... | collective-permute-start | bytes 3145736 | tf_op jit(solution)/shard_map/ppermute | solution.py:21
  50.4 2.7 copy-start.4
  50.4 4.2 copy-start.11
  50.5 4.3 %copy-start.9 = (f32[2,1024]{1,0:T(2,128)S(1)}, f32[2,1024]{1,0:T(2,128)}, u32[]{:S(2)}) copy-start(f32[2,1024]{1,0:T(2,128)} %param.17) | copy-start | bytes 24580
  53.1 36.0 %collective-permute-start.3 = (f32[3,1,128,1024]{3,2,1,0:T(8,128)}, f32[3,1,128,1024]{3,2,1,0:T(8,128)}, u32[]{:S(2)}, u32[]{:S(2)}) collective-permute-start(f32[3,1,128,1024]{3,2,1,0:T(8,128)} %get-tuple-element.10), channel_id=1, source_target_pairs={{1,0},{2,1},{3,2},{4,3},{5,4},{6,5},{7,6},{0,7},{9,8},{10,9},{11,1... | collective-permute-start | bytes 4718600 | tf_op jit(solution)/shard_map/ppermute | solution.py:21
  54.6 36.5 %collective-permute-start.2 = (f32[3,1,128,1024]{3,2,1,0:T(8,128)}, f32[3,1,128,1024]{3,2,1,0:T(8,128)}, u32[]{:S(2)}, u32[]{:S(2)}) collective-permute-start(f32[3,1,128,1024]{3,2,1,0:T(8,128)} %get-tuple-element.9), channel_id=1, source_target_pairs={{0,1},{1,2},{2,3},{3,4},{4,5},{5,6},{6,7},{7,0},{8,9},{9,10},{10,1... | collective-permute-start | bytes 4718600 | tf_op jit(solution)/shard_map/ppermute | solution.py:19
  97.7 6.5 %copy-start.8 = (f32[1,3,4,128,128]{4,3,2,1,0:T(8,128)S(1)}, f32[1,3,4,128,128]{4,3,2,1,0:T(8,128)}, u32[]{:S(2)}) copy-start(f32[1,3,4,128,128]{4,3,2,1,0:T(8,128)} %param.14) | copy-start | bytes 2359300
  110.2 5.0 %copy-start.10 = (s32[1,3,8]{2,0,1:T(1,128)S(1)}, s32[1,3,8]{2,0,1:T(1,128)}, u32[]{:S(2)}) copy-start(s32[1,3,8]{2,0,1:T(1,128)} %param.15) | copy-start | bytes 292
  111.3 40.1 %copy-start.13 = (s32[1,3]{1,0:T(1,128)S(1)}, s32[1,3]{1,0:T(1,128)}, u32[]{:S(2)}) copy-start(s32[1,3]{1,0:T(1,128)} %param.16) | copy-start | bytes 40
  111.6 21.5 %collective-permute-start.5 = (bf16[1,3,128,1024]{3,2,1,0:T(8,128)(2,1)S(1)}, bf16[1,3,128,1024]{3,2,1,0:T(8,128)(2,1)}, u32[]{:S(2)}, u32[]{:S(2)}) collective-permute-start(bf16[1,3,128,1024]{3,2,1,0:T(8,128)(2,1)S(1)} %fusion.83), channel_id=1, source_target_pairs={{8,0},{16,8},{24,16},{0,24},{9,1},{17,9},{25,17},{1,25},{10,2},{18... | collective-permute-start | bytes 2359304 | tf_op jit(solution)/shard_map/ppermute | solution.py:21
  115.1 33.3 %collective-permute-start.4 = (bf16[1,3,128,1024]{3,2,1,0:T(8,128)(2,1)S(1)}, bf16[1,3,128,1024]{3,2,1,0:T(8,128)(2,1)}, u32[]{:S(2)}, u32[]{:S(2)}) collective-permute-start(bf16[1,3,128,1024]{3,2,1,0:T(8,128)(2,1)S(1)} %fusion.83), channel_id=1, source_target_pairs={{0,8},{8,16},{16,24},{24,0},{1,9},{9,17},{17,25},{25,1},{2,10},{10... | collective-permute-start | bytes 2359304 | tf_op jit(solution)/shard_map/ppermute | solution.py:19
  115.3 36.2 %copy-start.2 = (f32[3,1024,128,1]{1,2,3,0:T(8,128)S(1)}, f32[3,1024,128,1]{1,2,3,0:T(8,128)}, u32[]{:S(2)}) copy-start(f32[3,1024,128,1]{1,2,3,0:T(8,128)} %copy-done.1) | copy-start | bytes 4718596
  150.9 17.6 %collective-permute-start.7 = (bf16[3,1,128,1024]{3,2,1,0:T(8,128)(2,1)}, bf16[3,1,128,1024]{3,2,1,0:T(8,128)(2,1)}, u32[]{:S(2)}, u32[]{:S(2)}) collective-permute-start(bf16[3,1,128,1024]{3,2,1,0:T(8,128)(2,1)} %get-tuple-element.12), channel_id=1, source_target_pairs={{1,0},{2,1},{3,2},{4,3},{5,4},{6,5},{7,6},{0,7},{9,8},{10,9},{11,1... | collective-permute-start | bytes 2359304 | tf_op jit(solution)/shard_map/ppermute | solution.py:21
  150.9 20.8 %collective-permute-start.6 = (bf16[3,1,128,1024]{3,2,1,0:T(8,128)(2,1)}, bf16[3,1,128,1024]{3,2,1,0:T(8,128)(2,1)}, u32[]{:S(2)}, u32[]{:S(2)}) collective-permute-start(bf16[3,1,128,1024]{3,2,1,0:T(8,128)(2,1)} %get-tuple-element.11), channel_id=1, source_target_pairs={{0,1},{1,2},{2,3},{3,4},{4,5},{5,6},{6,7},{7,0},{8,9},{9,10},{10,1... | collective-permute-start | bytes 2359304 | tf_op jit(solution)/shard_map/ppermute | solution.py:19
  259.9 13.5 %copy-start.3 = (f32[3,1024,128,1]{1,2,3,0:T(8,128)S(1)}, f32[3,1024,128,1]{1,2,3,0:T(8,128)}, u32[]{:S(2)}) copy-start(f32[3,1024,128,1]{1,2,3,0:T(8,128)} %copy-done.1) | copy-start | bytes 4718596
  285.2 75.2 %copy-start.12 = (s32[1,2,4]{2,1,0:T(2,128)S(1)}, s32[1,2,4]{2,1,0:T(2,128)}, u32[]{:S(2)}) copy-start(s32[1,2,4]{2,1,0:T(2,128)} %param.22) | copy-start | bytes 100
  285.2 37.2 %collective-permute-start.9 = (f32[1,3,128,1024]{3,2,1,0:T(8,128)}, f32[1,3,128,1024]{3,2,1,0:T(8,128)S(1)}, u32[]{:S(2)}, u32[]{:S(2)}) collective-permute-start(f32[1,3,128,1024]{3,2,1,0:T(8,128)} %bitcast.139), channel_id=1, source_target_pairs={{8,0},{16,8},{24,16},{0,24},{9,1},{17,9},{25,17},{1,25},{10,2},{18... | collective-permute-start | bytes 4718600 | tf_op jit(solution)/shard_map/ppermute | solution.py:21
  287.2 66.6 %collective-permute-start.8 = (f32[1,3,128,1024]{3,2,1,0:T(8,128)}, f32[1,3,128,1024]{3,2,1,0:T(8,128)S(1)}, u32[]{:S(2)}, u32[]{:S(2)}) collective-permute-start(f32[1,3,128,1024]{3,2,1,0:T(8,128)} %bitcast.140), channel_id=1, source_target_pairs={{0,8},{8,16},{16,24},{24,0},{1,9},{9,17},{17,25},{25,1},{2,10},{10... | collective-permute-start | bytes 4718600 | tf_op jit(solution)/shard_map/ppermute | solution.py:19
  322.3 35.2 %copy-start.6 = (f32[1,3,128,1024]{3,2,1,0:T(8,128)}, f32[1,3,128,1024]{3,2,1,0:T(8,128)S(1)}, u32[]{:S(2)}) copy-start(f32[1,3,128,1024]{3,2,1,0:T(8,128)S(1)} %collective-permute-done.9) | copy-start | bytes 4718596
  353.9 3.7 copy-start.7
  357.6 37.7 %collective-permute-start.11 = (f32[3,1,128,1024]{3,2,1,0:T(8,128)}, f32[3,1,128,1024]{3,2,1,0:T(8,128)}, u32[]{:S(2)}, u32[]{:S(2)}) collective-permute-start(f32[3,1,128,1024]{3,2,1,0:T(8,128)} %get-tuple-element.8), channel_id=1, source_target_pairs={{1,0},{2,1},{3,2},{4,3},{5,4},{6,5},{7,6},{0,7},{9,8},{10,9},{11,1... | collective-permute-start | bytes 4718600 | tf_op jit(solution)/shard_map/ppermute | solution.py:21
  360.4 36.3 %collective-permute-start.10 = (f32[3,1,128,1024]{3,2,1,0:T(8,128)}, f32[3,1,128,1024]{3,2,1,0:T(8,128)}, u32[]{:S(2)}, u32[]{:S(2)}) collective-permute-start(f32[3,1,128,1024]{3,2,1,0:T(8,128)} %get-tuple-element.7), channel_id=1, source_target_pairs={{0,1},{1,2},{2,3},{3,4},{4,5},{5,6},{6,7},{7,0},{8,9},{9,10},{10,1... | collective-permute-start | bytes 4718600 | tf_op jit(solution)/shard_map/ppermute | solution.py:19
  (2 other events, 2.3 us)
where the time goes:
time: 420 us; the launch traced here: 418 us
  waiting for transfers between devices  229 us (55%)
  local copies, waits for them, and re-layouts  82.5 us (20%)
  matrix products  68.8 us (16%)
  other arithmetic  22 us (5%)
  starting transfers between devices  15.6 us (4%)
    ppermute x6, waiting for transfers between devices, with_halo(): lax.ppermute(head, axis, [((i + 1) % count, i) for i in range(count)])  152 us
    ppermute x6, waiting for transfers between devices, with_halo(): lax.ppermute(tail, axis, [(i, (i + 1) % count) for i in range(count)])  77.7 us
    unnamed x32, local copies, waits for them, and re-layouts  22 us
    sub x1, matrix products, shards(): raw_weights = jnp.exp(masked - highest)  15.3 us
    concatenate x3, other arithmetic, with_halo(): jnp.concatenate([lax.ppermute(tail, axis, [(i, (i + 1) % count) for i in...  14.4 us
    dot_general x1, matrix products, shards(): jnp.einsum('mhqk,mkhd->mqhd', weights, values, preferred_element_type=jnp...  12.7 us
    dot_general x1, matrix products, shards(): jnp.dot(padded_normed.reshape(-1, feature_width), qkv_weight[:, feature_w...  12.4 us
    ppermute x6, starting transfers between devices, with_halo(): lax.ppermute(head, axis, [((i + 1) % count, i) for i in range(count)])  12 us
  transfers between devices with their start and end apart: 12, of which 12 were waited for; matrix products, arithmetic and copies ran while one was open for 2% of the time, Pallas kernels for 0%

commit v1 on v0

v1 whole, which is shorter than its diff:
```python
import jax
import jax.numpy as jnp
from jax import lax
from jax.experimental import pallas as pl
from jax.experimental.pallas import tpu as pltpu
from jax.sharding import PartitionSpec as P

HEADS = 16


EPSILON = 1e-05

MESH = pl.DeviceIdType.MESH
VMEM_LIMIT = 60 * 1024 * 1024


def layer_norm(values, gain):
    centred = values - jnp.mean(values, axis=-1, keepdims=True)
    spread = jnp.mean(centred * centred, axis=-1, keepdims=True)
    return (centred * lax.rsqrt(spread + EPSILON) * gain).astype(jnp.bfloat16)


def gelu_exact(values):
    return 0.5 * values * (1.0 + lax.erf(values * 0.7071067811865476))


def table_slot(row, column, blocks):
    if 1 <= column <= blocks:
        return row * blocks + column - 1
    return 3 * blocks + (1, 0, 2)[row] * 2 + (0 if column == 0 else 1)


def find_slot(global_id, total_lon, blocks):
    band_here = lax.axis_index("lat")
    sector_here = lax.axis_index("lon")
    row = global_id // total_lon - band_here + 1
    column = (global_id % total_lon - sector_here * blocks + 1 + total_lon) % total_lon
    side_row = jnp.where(row == 1, 0, jnp.where(row == 0, 1, 2))
    side = 3 * blocks + side_row * 2 + jnp.where(column == 0, 0, 1)
    inside = jnp.logical_and(column >= 1, column <= blocks)
    return jnp.where(inside, row * blocks + column - 1, side)


class Halo:
    def __init__(self, source, table, send_sem, recv_sem, blocks, rows):
        self.blocks = blocks
        lat_count, lon_count = lax.axis_size("lat"), lax.axis_size("lon")
        lat, lon = lax.axis_index("lat"), lax.axis_index("lon")
        self.above, self.below = lat > 0, lat < lat_count - 1
        self.right = (lat, lax.rem(lon + 1, lon_count))
        self.left = (lat, lax.rem(lon + lon_count - 1, lon_count))
        self.down = (lax.rem(lat + 1, lat_count), lon)
        self.up = (lax.rem(lat + lat_count - 1, lat_count), lon)

        def own(block):
            return source.at[block]

        def slot(row, column):
            return table.at[table_slot(row, column, blocks)]

        def copy(src, dst, number, device):
            return pltpu.make_async_remote_copy(
                src_ref=src,
                dst_ref=dst,
                send_sem=send_sem.at[number],
                recv_sem=recv_sem.at[number],
                device_id=device,
                device_id_type=MESH,
            )

        last = blocks - 1
        self.edges = [
            copy(own(last), slot(1, 0), 0, self.right),
            copy(own(0), slot(1, blocks + 1), 1, self.left),
        ]
        self.downs = [copy(own(j), slot(0, 1 + j), 2 + j, self.down) for j in range(blocks)]
        self.ups = [copy(own(j), slot(2, 1 + j), 2 + blocks + j, self.up) for j in range(blocks)]
        base = 2 + 2 * blocks
        self.corners_above = [
            copy(slot(0, blocks), slot(0, 0), base, self.right),
            copy(slot(0, 1), slot(0, blocks + 1), base + 1, self.left),
        ]
        self.corners_below = [
            copy(slot(2, blocks), slot(2, 0), base + 2, self.right),
            copy(slot(2, 1), slot(2, blocks + 1), base + 3, self.left),
        ]
        self.border = [0, last] if blocks > 1 else [0]
        self.middle = [j for j in range(blocks) if j not in self.border]

    @staticmethod
    def count(blocks):
        return 6 + 2 * blocks

    def greet(self):
        barrier = pltpu.get_barrier_semaphore()
        for device in (self.left, self.right):
            pl.semaphore_signal(barrier, inc=1, device_id=device, device_id_type=MESH)

        @pl.when(self.above)
        def _():
            pl.semaphore_signal(barrier, inc=1, device_id=self.up, device_id_type=MESH)

        @pl.when(self.below)
        def _():
            pl.semaphore_signal(barrier, inc=1, device_id=self.down, device_id_type=MESH)

        bands = self.above.astype(jnp.int32) + self.below.astype(jnp.int32)
        pl.semaphore_wait(barrier, 2 + bands)

    def start(self):
        for edge in self.edges:
            edge.start()
        for j in self.border + self.middle:
            @pl.when(self.below)
            def _():
                self.downs[j].start()

            @pl.when(self.above)
            def _():
                self.ups[j].start()

    def forward(self):
        @pl.when(self.above)
        def _():
            for j in self.border:
                self.downs[j].wait_recv()
            for corner in self.corners_above:
                corner.start()

        @pl.when(self.below)
        def _():
            for j in self.border:
                self.ups[j].wait_recv()
            for corner in self.corners_below:
                corner.start()

    def wait_edges(self):
        for edge in self.edges:
            edge.wait_recv()

    def wait_above(self):
        @pl.when(self.above)
        def _():
            for j in self.middle:
                self.downs[j].wait_recv()

    def wait_below(self):
        @pl.when(self.below)
        def _():
            for j in self.middle:
                self.ups[j].wait_recv()

    def wait_corners(self):
        @pl.when(self.above)
        def _():
            for corner in self.corners_above:
                corner.wait_recv()

        @pl.when(self.below)
        def _():
            for corner in self.corners_below:
                corner.wait_recv()

    def finish(self):
        for edge in self.edges:
            edge.wait_send()

        @pl.when(self.above)
        def _():
            for sent in self.ups + self.corners_above:
                sent.wait_send()

        @pl.when(self.below)
        def _():
            for sent in self.downs + self.corners_below:
                sent.wait_send()


def interpolate(slot_ref, weight_ref, table, target, rows):
    total = None
    for k in range(weight_ref.shape[1]):
        block = table[slot_ref[target, k]]
        weight = weight_ref[target, k]
        high = weight.astype(jnp.bfloat16)
        low = (weight - high.astype(jnp.float32)).astype(jnp.bfloat16)
        both = jnp.dot(
            jnp.concatenate([high, low], axis=0), block, preferred_element_type=jnp.float32
        )
        term = both[:rows] + both[rows:]
        total = term if total is None else total + term
    return total


def lift_kernel(
    blocks, rows,
    slot_ref, grid_ref, weight_ref, gain_ref, mesh_in_ref, normed_ref, table, send_sem, recv_sem,
):
    halo = Halo(grid_ref, table, send_sem, recv_sem, blocks, rows)
    halo.greet()
    halo.start()
    table[pl.ds(blocks, blocks)] = grid_ref[...]
    halo.forward()
    halo.wait_edges()
    halo.wait_above()
    halo.wait_below()
    halo.wait_corners()

    @pl.loop(0, weight_ref.shape[0])
    def _(target):
        total = interpolate(slot_ref, weight_ref, table, target, rows)
        mesh_in_ref[target] = total
        normed_ref[target] = layer_norm(total, gain_ref[0:1, :])

    halo.finish()


def return_kernel(
    blocks, rows,
    slot_ref, mesh_ref, weight_ref, out_ref, table, send_sem, recv_sem,
):
    halo = Halo(mesh_ref, table, send_sem, recv_sem, blocks, rows)
    halo.greet()
    halo.start()
    table[pl.ds(blocks, blocks)] = mesh_ref[...]
    halo.forward()
    halo.wait_edges()
    halo.wait_above()
    halo.wait_below()
    halo.wait_corners()

    @pl.loop(0, weight_ref.shape[0])
    def _(target):
        total = interpolate(slot_ref, weight_ref, table, target, rows)
        out_ref[target] = total

    halo.finish()


def attention_kernel(
    blocks, rows, tile,
    slot_ref, count_ref, normed_ref, weight_ref, mixed_ref,
    table, queries, key_value, send_sem, recv_sem,
):
    width = normed_ref.shape[2]
    pair = 2 * (width // HEADS)
    halo = Halo(normed_ref, table, send_sem, recv_sem, blocks, rows)
    halo.greet()
    halo.start()
    scale = (width // HEADS) ** (-0.5)

    @pl.loop(0, width // tile)
    def _(step):
        columns = pl.ds(pl.multiple_of(step * tile, tile), tile)
        product = jnp.dot(
            normed_ref[...].reshape(blocks * rows, width),
            weight_ref[:, columns],
            preferred_element_type=jnp.float32,
        )
        product = product.astype(jnp.bfloat16) * jnp.bfloat16(scale)
        queries[:, :, columns] = product.reshape(blocks, rows, tile)

    def project(source, first, many):
        @pl.loop(0, 2 * width // tile)
        def _(step):
            columns = pl.ds(pl.multiple_of(step * tile, tile), tile)
            taken = pl.ds(pl.multiple_of(width + step * tile, tile), tile)
            product = jnp.dot(
                source[...].reshape(many * rows, width),
                weight_ref[:, taken],
                preferred_element_type=jnp.float32,
            )
            product = product.astype(jnp.bfloat16).reshape(many, rows, tile)
            key_value[pl.ds(first, many), :, columns] = product

    def project_slots(first, many):
        project(table.at[pl.ds(first, many)], first, many)

    project(normed_ref, blocks, blocks)
    halo.wait_edges()
    halo.forward()
    project_slots(3 * blocks, 2)
    halo.wait_above()
    project_slots(0, blocks)
    halo.wait_below()
    project_slots(2 * blocks, blocks)
    halo.wait_corners()
    project_slots(3 * blocks + 2, 4)

    slots = slot_ref.shape[1]
    lane = lax.broadcasted_iota(jnp.int32, (rows, pair), 1)
    first_half = lane < pair // 2
    key_block = lax.broadcasted_iota(jnp.int32, (1, slots * rows), 1) // rows

    @pl.loop(0, blocks)
    def _(target):
        live = key_block < count_ref[0, target]
        places = [slot_ref[target, s] for s in range(slots)]

        @pl.loop(0, width // pair)
        def _(group):
            columns = pl.ds(pl.multiple_of(group * pair, pair), pair)
            value_columns = pl.ds(pl.multiple_of(width + group * pair, pair), pair)
            query = queries[target, :, columns]
            zero = jnp.zeros_like(query)
            both = jnp.concatenate(
                [jnp.where(first_half, query, zero), jnp.where(first_half, zero, query)], axis=0
            )
            keys = jnp.concatenate([key_value[place, :, columns] for place in places], axis=0)
            values = jnp.concatenate([key_value[place, :, value_columns] for place in places], axis=0)
            scores = lax.dot_general(
                both, keys, (((1,), (1,)), ((), ())), preferred_element_type=jnp.float32
            )
            masked = jnp.where(live, scores, -1e30)
            raw = jnp.exp(masked - jnp.max(masked, axis=-1, keepdims=True))
            total = jnp.sum(raw, axis=-1, keepdims=True)
            mixed = jnp.dot(
                raw.astype(jnp.bfloat16), values, preferred_element_type=jnp.float32
            ) / total
            mixed_ref[target, :, columns] = jnp.where(
                first_half, mixed[:rows], mixed[rows:]
            ).astype(jnp.bfloat16)

    halo.finish()


def in_vmem(count):
    return [pl.BlockSpec(memory_space=pltpu.VMEM)] * count


def in_smem(count):
    return [pl.BlockSpec(memory_space=pltpu.SMEM)] * count


def halo_scratch(blocks, rows, width):
    count = Halo.count(blocks)
    slots = 3 * (blocks + 2)
    return (
        [pltpu.VMEM((slots, rows, width), jnp.bfloat16)],
        [pltpu.SemaphoreType.DMA((count,)), pltpu.SemaphoreType.DMA((count,))],
    )


def parameters(number):
    return pltpu.CompilerParams(
        collective_id=number, has_side_effects=True, vmem_limit_bytes=VMEM_LIMIT
    )


def shards(
    grid_feats,
    lift_index,
    lift_weight,
    window_index,
    window_count,
    norm_gains,
    qkv_weight,
    out_weight,
    up_weight,
    down_weight,
    return_index,
    return_weight,
):
    lon_count = lax.axis_size("lon")
    grid_blocks = grid_feats.shape[1]
    mesh_blocks = lift_index.shape[1]
    rows = grid_feats.shape[2]
    width = grid_feats.shape[3]
    grid_lon = grid_blocks * lon_count
    mesh_lon = mesh_blocks * lon_count

    grid_table, grid_sems = halo_scratch(grid_blocks, rows, width)
    mesh_table, mesh_sems = halo_scratch(mesh_blocks, rows, width)
    mesh_in, normed = pl.pallas_call(
        lambda *refs: lift_kernel(grid_blocks, rows, *refs),
        out_shape=(
            jax.ShapeDtypeStruct((mesh_blocks, rows, width), jnp.float32),
            jax.ShapeDtypeStruct((mesh_blocks, rows, width), jnp.bfloat16),
        ),
        in_specs=in_smem(1) + in_vmem(3),
        out_specs=tuple(in_vmem(2)),
        scratch_shapes=grid_table + grid_sems,
        compiler_params=parameters(0),
    )(
        find_slot(lift_index[0], grid_lon, grid_blocks),
        grid_feats[0].astype(jnp.bfloat16),
        lift_weight[0],
        norm_gains,
    )
    tile = min(512, width)
    mixed = pl.pallas_call(
        lambda *refs: attention_kernel(mesh_blocks, rows, tile, *refs),
        out_shape=jax.ShapeDtypeStruct((mesh_blocks, rows, width), jnp.bfloat16),
        in_specs=in_smem(2) + in_vmem(2),
        out_specs=in_vmem(1)[0],
        scratch_shapes=mesh_table
        + [
            pltpu.VMEM((mesh_blocks, rows, width), jnp.bfloat16),
            pltpu.VMEM((3 * (mesh_blocks + 2), rows, 2 * width), jnp.bfloat16),
        ]
        + mesh_sems,
        compiler_params=parameters(1),
    )(find_slot(window_index[0], mesh_lon, mesh_blocks), window_count, normed, qkv_weight)
    mixed = mixed.reshape(-1, width)
    after_attention = mesh_in.reshape(-1, width) + jnp.dot(
        mixed, out_weight, preferred_element_type=jnp.float32
    )
    normed_again = layer_norm(after_attention, norm_gains[1])
    hidden_units = gelu_exact(
        jnp.dot(normed_again, up_weight, preferred_element_type=jnp.float32)
    ).astype(jnp.bfloat16)
    mesh_out = after_attention + jnp.dot(
        hidden_units, down_weight, preferred_element_type=jnp.float32
    )
    grid_out = pl.pallas_call(
        lambda *refs: return_kernel(mesh_blocks, rows, *refs),
        out_shape=jax.ShapeDtypeStruct((grid_blocks, rows, width), jnp.float32),
        in_specs=in_smem(1) + in_vmem(2),
        out_specs=in_vmem(1)[0],
        scratch_shapes=mesh_table + mesh_sems,
        compiler_params=parameters(2),
    )(
        find_slot(return_index[0], mesh_lon, mesh_blocks),
        mesh_out.astype(jnp.bfloat16).reshape(mesh_blocks, rows, width),
        return_weight[0],
    )
    return grid_out.reshape(1, grid_blocks, rows, width)


def solution(mesh):
    placed = (
        P("lat", "lon", None, None),
        P("lat", "lon", None),
        P("lat", "lon", None, None, None),
        P("lat", "lon", None),
        P("lat", "lon"),
        P(),
        P(),
        P(),
        P(),
        P(),
        P("lat", "lon", None),
        P("lat", "lon", None, None, None),
    )
    return jax.shard_map(
        shards, mesh=mesh, in_specs=placed, out_specs=P("lat", "lon", None, None), check_vma=False
    )
```

time: 420 us -> 135 us (0.32)
  the two profiles are of different devices: /device:TPU:0 before, /device:TPU:16 now
where the time goes in v1:
time: 135 us
  Pallas kernels  114 us (84%)
  matrix products  11 us (8%)
  other arithmetic  6.42 us (5%)
  local copies, waits for them, and re-layouts  3.5 us (3%)
    pallas_call x1, Pallas kernels, shards(): pl.pallas_call(lambda *refs: attention_kernel(mesh_blocks, rows, tile, *r...  50.9 us
    pallas_call x1, Pallas kernels, shards(): pl.pallas_call(lambda *refs: return_kernel(mesh_blocks, rows, *refs), out...  31.5 us
    pallas_call x1, Pallas kernels, shards(): pl.pallas_call(lambda *refs: lift_kernel(grid_blocks, rows, *refs), out_s...  31.1 us
    dot_general x1, matrix products, shards(): jnp.dot(hidden_units, down_weight, preferred_element_type=jnp.float32)  8.81 us
    unnamed x11, local copies, waits for them, and re-layouts  3.49 us

profile of v1, /device:TPU:16, one launch (start us, length us, event | category | flops | bytes accessed | tf_op | source)
XLA Modules:
  0.0 134.5 jit_solution(10944970319022161578)
XLA Ops:
  0.0 0.0 copy-start
  0.0 0.8 broadcast_remainder_fusion
  0.8 0.7 sign_compare_fusion
  1.5 0.6 add_select_fusion.6.refs_0_
  2.1 1.3 add_select_fusion.7.refs_0_
  3.4 2.1 %convert_bitcast_fusion.refs_1_ = bf16[2,128,1024]{2,1,0:T(8,128)(2,1)} fusion(f32[1,2,128,1024]{3,2,1,0:T(8,128)} %param.12), kind=kLoop, calls=%fused_computation.10 | loop fusion | flops 262144 | bytes 1572864 | tf_op jit(solution)/shard_map/convert_element_type | solution.py:385
  5.5 31.1 %shard_map.118 = (f32[3,128,1024]{2,1,0:T(8,128)}, bf16[3,128,1024]{2,1,0:T(8,128)(2,1)}) custom-call(s32[3,4]{1,0:T(4,128)} %add_select_fusion.7.refs_0_, bf16[2,128,1024]{2,1,0:T(8,128)(2,1)} %convert_bitcast_fusion.refs_1_, f32[3,4,128,128]{3,2,1,0:T(8,128)} %bitcast.85, f32[2,1024]{1,0:T(2,128)} %refs_3_.2), custom_call_target="tpu_custom_call" | custom-call | tf_op jit(solution)/shard_map/pallas_call | solution.py:373
  36.6 0.0 copy-start.4
  36.6 50.9 %shard_map.119 = bf16[3,128,1024]{2,1,0:T(8,128)(2,1)} custom-call(s32[3,8]{1,0:T(4,128)} %add_select_fusion.6.refs_0_, s32[1,3]{1,0:T(1,128)} %refs_1_.1, bf16[3,128,1024]{2,1,0:T(8,128)(2,1)} %get-tuple-element.8.refs_2_, bf16[1024,3072]{1,0:T(8,128)(2,1)} %refs_3_.3), custom_call_target="tpu_custom_call" | custom-call | tf_op jit(solution)/shard_map/pallas_call | solution.py:390
  87.5 0.0 copy-done
  87.5 0.0 copy-done.4
  87.5 0.0 copy-start.2
  87.6 2.2 %fusion.33 = (f32[384]{0:T(512)S(1)}, f32[384,1024]{1,0:T(8,128)S(1)}) fusion(bf16[384,1024]{1,0:T(8,128)(2,1)} %bitcast.84, bf16[1024,1024]{1,0:T(8,128)(2,1)S(1)} %copy-done, f32[3,128,1024]{2,1,0:T(8,128)S(1)} %copy-done.4), kind=kOutput, calls=%fused_computation.67 | convolution fusion | flops 806092416 | bytes 6030848 | tf_op jit(solution)/shard_map/dot_general | solution.py:404
  89.8 0.0 copy-start.1
  89.8 1.2 copy-done.1
  90.9 0.3 multiply_reduce_fusion
  91.2 0.0 copy-done.2
  91.3 0.0 copy-start.3
  91.3 8.8 %add_convert_fusion = bf16[384,1024]{1,0:T(8,128)(2,1)} fusion(f32[384,1024]{1,0:T(8,128)} %copy-done.1, bf16[2048,1024]{1,0:T(8,128)(2,1)} %param.21, bf16[1024,2048]{1,0:T(8,128)(2,1)} %param.20, f32[1024]{0:T(1024)S(1)} %bitcast.88, f32[384]{0:T(512)S(1)} %add_rsqrt_fusion, f32[384]{0:T(512)S(1)} %broadcast_multiply_fusion), kind=kOutput, calls=%fused_computation.2 | convolution fusion | flops 3227516928 | bytes 10755072 | tf_op jit(solution)/shard_map/dot_general | solution.py:411
  100.1 0.0 copy-done.3
  100.1 0.6 and_select_fusion.refs_0_
  100.7 31.5 %shard_map.120 = f32[2,128,1024]{2,1,0:T(8,128)} custom-call(s32[2,4]{1,0:T(2,128)} %and_select_fusion.refs_0_, bf16[3,128,1024]{2,1,0:T(8,128)(2,1)} %bitcast.86, f32[2,4,128,128]{3,2,1,0:T(8,128)} %bitcast.87), custom_call_target="tpu_custom_call" | custom-call | tf_op jit(solution)/shard_map/pallas_call | solution.py:414
  132.2 2.3 %copy.52 = f32[1,2,128,1024]{3,2,1,0:T(8,128)} copy(f32[1,2,128,1024]{3,2,1,0:T(8,128)} %bitcast.83) | data formatting | bytes 2097152
  (3 shorter events, 0.0 us)
Async XLA Ops:
  0.0 87.5 %copy-start = (bf16[1024,1024]{1,0:T(8,128)(2,1)S(1)}, bf16[1024,1024]{1,0:T(8,128)(2,1)}, u32[]{:S(2)}) copy-start(bf16[1024,1024]{1,0:T(8,128)(2,1)} %param.19) | copy-start | bytes 6291460
  36.6 50.9 %copy-start.4 = (f32[3,128,1024]{2,1,0:T(8,128)S(1)}, f32[3,128,1024]{2,1,0:T(8,128)}, u32[]{:S(2)}) copy-start(f32[3,128,1024]{2,1,0:T(8,128)} %get-tuple-element.7) | copy-start | bytes 4718596
  87.5 3.7 %copy-start.2 = (f32[2,1024]{1,0:T(2,128)S(1)}, f32[2,1024]{1,0:T(2,128)}, u32[]{:S(2)}) copy-start(f32[2,1024]{1,0:T(2,128)} %refs_3_.2) | copy-start | bytes 24580
  89.8 1.2 copy-start.1
  91.3 8.8 %copy-start.3 = (s32[1,2,4]{2,1,0:T(2,128)S(1)}, s32[1,2,4]{2,1,0:T(2,128)}, u32[]{:S(2)}) copy-start(s32[1,2,4]{2,1,0:T(2,128)} %param.22) | copy-start | bytes 100

commit v2 on v1

v2 whole, which is shorter than its diff:
```python
import jax
import jax.numpy as jnp
from jax import lax
from jax.experimental import pallas as pl
from jax.experimental.pallas import tpu as pltpu
from jax.sharding import PartitionSpec as P

HEADS = 16


EPSILON = 1e-05

MESH = pl.DeviceIdType.MESH
VMEM_LIMIT = 60 * 1024 * 1024


def layer_norm(values, gain):
    centred = values - jnp.mean(values, axis=-1, keepdims=True)
    spread = jnp.mean(centred * centred, axis=-1, keepdims=True)
    return (centred * lax.rsqrt(spread + EPSILON) * gain).astype(jnp.bfloat16)


def gelu_exact(values):
    return 0.5 * values * (1.0 + lax.erf(values * 0.7071067811865476))


def find_slot(global_id, total_lon, blocks):
    sector_here = lax.axis_index("lon")
    odd = lax.rem(sector_here, 2)
    source_band = lax.div(global_id, total_lon)
    row = source_band - lax.axis_index("lat")
    column = lax.rem(
        global_id - source_band * total_lon - sector_here * blocks + 1 + total_lon, total_lon
    )
    band = jnp.where(row < 0, 0, 1)
    place = column - 1
    side = jnp.where(column == 0, 0, 1)
    outside = jnp.logical_or(column == 0, column == blocks + 1)
    first = odd * (blocks - 1)
    corner = jnp.where(side == odd, blocks + 8 + 2 * (blocks - 2) + band, blocks + 6 + band)
    border = jnp.where(place == first, blocks + 2 + band, blocks + 4 + band)
    between = blocks + 8 + band * (blocks - 2) + place - 1
    middle = jnp.logical_and(place > 0, place < blocks - 1)
    other = jnp.where(outside, corner, jnp.where(middle, between, border))
    same = jnp.where(outside, blocks + side, place)
    found = jnp.where(row == 0, same, other)
    return jnp.minimum(jnp.maximum(found, 0), 3 * (blocks + 2) - 1)


class Halo:
    def __init__(self, source, table, send_sem, recv_sem, blocks):
        lat_count, lon_count = lax.axis_size("lat"), lax.axis_size("lon")
        lat, lon = lax.axis_index("lat"), lax.axis_index("lon")
        odd = lax.rem(lon, 2)
        self.above, self.below = lat > 0, lat < lat_count - 1
        self.outer = (lat, lax.rem(lon + 2 * odd - 1 + lon_count, lon_count))
        self.inner = (lat, lax.rem(lon + 1 - 2 * odd + lon_count, lon_count))
        self.down = (lax.rem(lat + 1, lat_count), lon)
        self.up = (lax.rem(lat + lat_count - 1, lat_count), lon)
        first = odd * (blocks - 1)
        second = blocks - 1 - first
        number = 0

        def copy(src, dst, device):
            nonlocal number
            number += 1
            return pltpu.make_async_remote_copy(
                src_ref=src,
                dst_ref=dst,
                send_sem=send_sem.at[number - 1],
                recv_sem=recv_sem.at[number - 1],
                device_id=device,
                device_id_type=MESH,
            )

        self.edges = [
            copy(source.at[first], table.at[blocks + 1 - odd], self.outer),
            copy(source.at[second], table.at[blocks + odd], self.inner),
        ]
        ends = [(first, blocks + 2), (second, blocks + 4)]
        self.vertical = []
        for place, slot in ends:
            self.vertical.append(
                (
                    copy(source.at[place], table.at[slot], self.down),
                    copy(source.at[place], table.at[slot + 1], self.up),
                )
            )
        between = blocks + 8
        for place in range(1, blocks - 1):
            slot = between + place - 1
            self.vertical.append(
                (
                    copy(source.at[place], table.at[slot], self.down),
                    copy(source.at[place], table.at[slot + blocks - 2], self.up),
                )
            )
        last = between + 2 * (blocks - 2)
        self.corners = [
            [
                copy(table.at[blocks + 2 + band], table.at[last + band], self.outer)
                for band in (0, 1)
            ],
            [
                copy(table.at[blocks + 4 + band], table.at[blocks + 6 + band], self.inner)
                for band in (0, 1)
            ],
        ]

    @staticmethod
    def count(blocks):
        return 6 + 2 * blocks

    def greet(self):
        barrier = pltpu.get_barrier_semaphore()
        for device in (self.outer, self.inner):
            pl.semaphore_signal(barrier, inc=1, device_id=device, device_id_type=MESH)

        @pl.when(self.above)
        def _():
            pl.semaphore_signal(barrier, inc=1, device_id=self.up, device_id_type=MESH)

        @pl.when(self.below)
        def _():
            pl.semaphore_signal(barrier, inc=1, device_id=self.down, device_id_type=MESH)

        bands = self.above.astype(jnp.int32) + self.below.astype(jnp.int32)
        pl.semaphore_wait(barrier, 2 + bands)

    def start(self):
        for edge in self.edges[:1]:
            edge.start()
        for down, up in self.vertical:
            @pl.when(self.below)
            def _():
                down.start()

            @pl.when(self.above)
            def _():
                up.start()
        for edge in self.edges[1:]:
            edge.start()

    def forward(self, order):
        down, up = self.vertical[order]
        above, below = self.corners[order]

        @pl.when(self.above)
        def _():
            down.wait_recv()
            above.start()

        @pl.when(self.below)
        def _():
            up.wait_recv()
            below.start()

    def wait_edges(self):
        for edge in self.edges:
            edge.wait_recv()

    def wait_corners(self, order):
        above, below = self.corners[order]

        @pl.when(self.above)
        def _():
            above.wait_recv()

        @pl.when(self.below)
        def _():
            below.wait_recv()

    def wait_between(self):
        for down, up in self.vertical[2:]:
            @pl.when(self.above)
            def _():
                down.wait_recv()

            @pl.when(self.below)
            def _():
                up.wait_recv()

    def receive(self, blocks, work):
        self.forward(0)
        self.wait_edges()
        work(blocks, 4)
        self.forward(1)
        self.wait_corners(1)
        work(blocks + 4, 4)
        self.wait_between()
        self.wait_corners(0)
        work(blocks + 8, 2 * (blocks - 2) + 2)

    def finish(self):
        for edge in self.edges:
            edge.wait_send()

        @pl.when(self.above)
        def _():
            for _, up in self.vertical:
                up.wait_send()
            for above, _ in self.corners:
                above.wait_send()

        @pl.when(self.below)
        def _():
            for down, _ in self.vertical:
                down.wait_send()
            for _, below in self.corners:
                below.wait_send()


SPREAD = 20.0


def encode(values):
    return jnp.exp2(values * SPREAD).astype(jnp.bfloat16)


def decode(coded):
    return jnp.log2(coded.astype(jnp.float32)) * (1.0 / SPREAD)


def halves(values):
    high = values.astype(jnp.bfloat16)
    low = (values - high.astype(jnp.float32)).astype(jnp.bfloat16)
    return high, low


def lift_kernel(
    total_lon, blocks, rows,
    index_ref, grid_ref, weight_ref, gain_ref, mesh_in_ref, normed_ref,
    table, high_table, low_table, send_sem, recv_sem,
):
    halo = Halo(grid_ref, table, send_sem, recv_sem, blocks)
    halo.greet()
    halo.start()

    def unpack(source, start, first, many):
        @pl.loop(0, many)
        def _(block):
            high, low = halves(decode(source[start + block]))
            high_table[first + block] = high
            low_table[first + block] = low

    unpack(grid_ref, 0, 0, blocks)
    halo.receive(blocks, lambda first, many: unpack(table, first, first, many))

    @pl.loop(0, weight_ref.shape[0])
    def _(target):
        total = None
        for k in range(weight_ref.shape[1]):
            place = find_slot(index_ref[target, k], total_lon, blocks)
            high, low = halves(weight_ref[target, k])
            both = jnp.dot(
                jnp.concatenate([high, low], axis=0),
                high_table[place],
                preferred_element_type=jnp.float32,
            )
            rest = jnp.dot(high, low_table[place], preferred_element_type=jnp.float32)
            term = both[:rows] + (both[rows:] + rest)
            total = term if total is None else total + term
        mesh_in_ref[target] = total
        normed_ref[target] = layer_norm(total, gain_ref[0:1, :])

    halo.finish()


def return_kernel(
    total_lon, blocks, rows,
    index_ref, mesh_ref, weight_ref, out_ref, table, send_sem, recv_sem,
):
    halo = Halo(mesh_ref, table, send_sem, recv_sem, blocks)
    halo.greet()
    halo.start()
    table[pl.ds(0, blocks)] = mesh_ref[...]
    halo.receive(blocks, lambda first, many: None)

    @pl.loop(0, weight_ref.shape[0])
    def _(target):
        total = None
        for k in range(weight_ref.shape[1]):
            place = find_slot(index_ref[target, k], total_lon, blocks)
            high, low = halves(weight_ref[target, k])
            both = jnp.dot(
                jnp.concatenate([high, low], axis=0),
                table[place],
                preferred_element_type=jnp.float32,
            )
            term = both[:rows] + both[rows:]
            total = term if total is None else total + term
        out_ref[target] = total

    halo.finish()


def attention_kernel(
    total_lon, blocks, rows, tile,
    index_ref, count_ref, normed_ref, weight_ref, mixed_ref,
    table, queries, key_value, send_sem, recv_sem,
):
    width = normed_ref.shape[2]
    pair = 2 * (width // HEADS)
    halo = Halo(normed_ref, table, send_sem, recv_sem, blocks)
    halo.greet()
    halo.start()
    scale = (width // HEADS) ** (-0.5)

    @pl.loop(0, width // tile)
    def _(step):
        columns = pl.ds(pl.multiple_of(step * tile, tile), tile)
        product = jnp.dot(
            normed_ref[...].reshape(blocks * rows, width),
            weight_ref[:, columns],
            preferred_element_type=jnp.float32,
        )
        product = product.astype(jnp.bfloat16) * jnp.bfloat16(scale)
        queries[:, :, columns] = product.reshape(blocks, rows, tile)

    def project(source, first, many):
        @pl.loop(0, 2 * width // tile)
        def _(step):
            columns = pl.ds(pl.multiple_of(step * tile, tile), tile)
            taken = pl.ds(pl.multiple_of(width + step * tile, tile), tile)
            product = jnp.dot(
                source[...].reshape(many * rows, width),
                weight_ref[:, taken],
                preferred_element_type=jnp.float32,
            )
            product = product.astype(jnp.bfloat16).reshape(many, rows, tile)
            key_value[pl.ds(first, many), :, columns] = product

    def project_slots(first, many):
        project(table.at[pl.ds(first, many)], first, many)

    project(normed_ref, 0, blocks)
    halo.receive(blocks, project_slots)

    slots = index_ref.shape[1]
    lane = lax.broadcasted_iota(jnp.int32, (rows, pair), 1)
    first_half = lane < pair // 2
    key_block = lax.broadcasted_iota(jnp.int32, (1, slots * rows), 1) // rows

    @pl.loop(0, blocks)
    def _(target):
        live = key_block < count_ref[0, target]
        places = [find_slot(index_ref[target, s], total_lon, blocks) for s in range(slots)]

        def attend(group):
            columns = pl.ds(pl.multiple_of(group * pair, pair), pair)
            value_columns = pl.ds(pl.multiple_of(width + group * pair, pair), pair)
            query = queries[target, :, columns]
            zero = jnp.zeros_like(query)
            both = jnp.concatenate(
                [jnp.where(first_half, query, zero), jnp.where(first_half, zero, query)], axis=0
            )
            keys = jnp.concatenate([key_value[place, :, columns] for place in places], axis=0)
            values = jnp.concatenate([key_value[place, :, value_columns] for place in places], axis=0)
            scores = lax.dot_general(
                both, keys, (((1,), (1,)), ((), ())), preferred_element_type=jnp.float32
            )
            masked = jnp.where(live, scores, -1e30)
            raw = jnp.exp(masked - jnp.max(masked, axis=-1, keepdims=True))
            total = jnp.sum(raw, axis=-1, keepdims=True)
            mixed = jnp.dot(
                raw.astype(jnp.bfloat16), values, preferred_element_type=jnp.float32
            ) / total
            mixed_ref[target, :, columns] = jnp.where(
                first_half, mixed[:rows], mixed[rows:]
            ).astype(jnp.bfloat16)

        @pl.loop(0, width // pair // 2)
        def _(step):
            attend(2 * step)
            attend(2 * step + 1)

    halo.finish()


def in_vmem(count):
    return [pl.BlockSpec(memory_space=pltpu.VMEM)] * count


def in_smem(count):
    return [pl.BlockSpec(memory_space=pltpu.SMEM)] * count


def halo_scratch(blocks, rows, width):
    count = Halo.count(blocks)
    slots = 3 * (blocks + 2)
    return (
        [pltpu.VMEM((slots, rows, width), jnp.bfloat16)],
        [pltpu.SemaphoreType.DMA((count,)), pltpu.SemaphoreType.DMA((count,))],
    )


def parameters(number):
    return pltpu.CompilerParams(
        collective_id=number, has_side_effects=True, vmem_limit_bytes=VMEM_LIMIT
    )


def shards(
    grid_feats,
    lift_index,
    lift_weight,
    window_index,
    window_count,
    norm_gains,
    qkv_weight,
    out_weight,
    up_weight,
    down_weight,
    return_index,
    return_weight,
):
    lon_count = lax.axis_size("lon")
    grid_blocks = grid_feats.shape[1]
    mesh_blocks = lift_index.shape[1]
    rows = grid_feats.shape[2]
    width = grid_feats.shape[3]
    grid_lon = grid_blocks * lon_count
    mesh_lon = mesh_blocks * lon_count

    grid_table, grid_sems = halo_scratch(grid_blocks, rows, width)
    mesh_table, mesh_sems = halo_scratch(mesh_blocks, rows, width)
    mesh_in, normed = pl.pallas_call(
        lambda *refs: lift_kernel(grid_lon, grid_blocks, rows, *refs),
        out_shape=(
            jax.ShapeDtypeStruct((mesh_blocks, rows, width), jnp.float32),
            jax.ShapeDtypeStruct((mesh_blocks, rows, width), jnp.bfloat16),
        ),
        in_specs=in_smem(1) + in_vmem(3),
        out_specs=tuple(in_vmem(2)),
        scratch_shapes=grid_table * 3 + grid_sems,
        compiler_params=parameters(0),
    )(
        lift_index[0],
        encode(grid_feats[0]),
        lift_weight[0],
        norm_gains,
    )
    tile = min(512, width)
    mixed = pl.pallas_call(
        lambda *refs: attention_kernel(mesh_lon, mesh_blocks, rows, tile, *refs),
        out_shape=jax.ShapeDtypeStruct((mesh_blocks, rows, width), jnp.bfloat16),
        in_specs=in_smem(2) + in_vmem(2),
        out_specs=in_vmem(1)[0],
        scratch_shapes=mesh_table
        + [
            pltpu.VMEM((mesh_blocks, rows, width), jnp.bfloat16),
            pltpu.VMEM((3 * (mesh_blocks + 2), rows, 2 * width), jnp.bfloat16),
        ]
        + mesh_sems,
        compiler_params=parameters(1),
    )(window_index[0], window_count, normed, qkv_weight)
    mixed = mixed.reshape(-1, width)
    after_attention = mesh_in.reshape(-1, width) + jnp.dot(
        mixed, out_weight, preferred_element_type=jnp.float32
    )
    normed_again = layer_norm(after_attention, norm_gains[1])
    hidden_units = gelu_exact(
        jnp.dot(normed_again, up_weight, preferred_element_type=jnp.float32)
    ).astype(jnp.bfloat16)
    mesh_out = after_attention + jnp.dot(
        hidden_units, down_weight, preferred_element_type=jnp.float32
    )
    grid_out = pl.pallas_call(
        lambda *refs: return_kernel(mesh_lon, mesh_blocks, rows, *refs),
        out_shape=jax.ShapeDtypeStruct((grid_blocks, rows, width), jnp.float32),
        in_specs=in_smem(1) + in_vmem(2),
        out_specs=in_vmem(1)[0],
        scratch_shapes=mesh_table + mesh_sems,
        compiler_params=parameters(2),
    )(
        return_index[0],
        mesh_out.astype(jnp.bfloat16).reshape(mesh_blocks, rows, width),
        return_weight[0],
    )
    return grid_out.reshape(1, grid_blocks, rows, width)


def solution(mesh):
    placed = (
        P("lat", "lon", None, None),
        P("lat", "lon", None),
        P("lat", "lon", None, None, None),
        P("lat", "lon", None),
        P("lat", "lon"),
        P(),
        P(),
        P(),
        P(),
        P(),
        P("lat", "lon", None),
        P("lat", "lon", None, None, None),
    )
    return jax.shard_map(
        shards, mesh=mesh, in_specs=placed, out_specs=P("lat", "lon", None, None), check_vma=False
    )
```

time: 135 us -> 116 us (0.86)
  the two profiles are of different devices: /device:TPU:16 before, /device:TPU:0 now
where the time goes in v2:
time: 116 us
  Pallas kernels  97 us (84%)
  matrix products  11 us (9%)
  local copies, waits for them, and re-layouts  5.33 us (5%)
  other arithmetic  2.64 us (2%)
    pallas_call x1, Pallas kernels, shards(): pl.pallas_call(lambda *refs: attention_kernel(mesh_lon, mesh_blocks, rows...  47.6 us
    pallas_call x1, Pallas kernels, shards(): pl.pallas_call(lambda *refs: return_kernel(mesh_lon, mesh_blocks, rows, *...  25.1 us
    pallas_call x1, Pallas kernels, shards(): pl.pallas_call(lambda *refs: lift_kernel(grid_lon, grid_blocks, rows, *re...  24.3 us
    dot_general x1, matrix products, shards(): jnp.dot(hidden_units, down_weight, preferred_element_type=jnp.float32)  8.81 us
    unnamed x13, local copies, waits for them, and re-layouts  5.33 us
    convert_element_type x1, other arithmetic, encode(): return jnp.exp2(values * SPREAD).astype(jnp.bfloat16)  2.33 us

profile of v2, /device:TPU:0, one launch (start us, length us, event | category | flops | bytes accessed | tf_op | source)
XLA Modules:
  0.0 116.1 jit_solution(1171199174594784932)
XLA Ops:
  0.0 0.0 copy-start
  0.0 0.0 copy-start.3
  0.0 2.3 %fusion.8.refs_1_ = bf16[2,128,1024]{2,1,0:T(8,128)(2,1)} fusion(f32[1,2,128,1024]{3,2,1,0:T(8,128)} %param.12), kind=kLoop, calls=%fused_computation.11 | loop fusion | flops 524288 | bytes 1572864 | tf_op jit(solution)/shard_map/convert_element_type | solution.py:217
  2.3 1.3 %copy.18 = s32[1,3,4]{2,1,0:T(4,128)} copy(s32[1,3,4]{2,0,1:T(1,128)} %param.13) | data formatting | bytes 96
  3.6 24.3 %shard_map.118 = (f32[3,128,1024]{2,1,0:T(8,128)}, bf16[3,128,1024]{2,1,0:T(8,128)(2,1)}) custom-call(s32[3,4]{1,0:T(4,128)} %bitcast.26, bf16[2,128,1024]{2,1,0:T(8,128)(2,1)} %fusion.8.refs_1_, f32[3,4,128,128]{3,2,1,0:T(8,128)} %bitcast.23, f32[2,1024]{1,0:T(2,128)} %refs_3_.2), custom_call_target="tpu_custom_call" | custom-call | tf_op jit(solution)/shard_map/pallas_call | solution.py:427
  27.9 0.0 copy-done.3
  27.9 0.6 copy.17
  28.5 0.0 copy-start.4
  28.5 47.6 %shard_map.119 = bf16[3,128,1024]{2,1,0:T(8,128)(2,1)} custom-call(s32[3,8]{1,0:T(4,128)} %bitcast.27, s32[1,3]{1,0:T(1,128)} %refs_1_.1, bf16[3,128,1024]{2,1,0:T(8,128)(2,1)} %get-tuple-element.8.refs_2_, bf16[1024,3072]{1,0:T(8,128)(2,1)} %refs_3_.3), custom_call_target="tpu_custom_call" | custom-call | tf_op jit(solution)/shard_map/pallas_call | solution.py:444
  76.1 0.0 copy-done
  76.1 0.0 copy-done.4
  76.1 0.0 copy-start.2
  76.1 2.2 %fusion.12 = (f32[384]{0:T(512)S(1)}, f32[384,1024]{1,0:T(8,128)S(1)}) fusion(bf16[384,1024]{1,0:T(8,128)(2,1)} %bitcast.22, bf16[1024,1024]{1,0:T(8,128)(2,1)S(1)} %copy-done, f32[3,128,1024]{2,1,0:T(8,128)S(1)} %copy-done.4), kind=kOutput, calls=%fused_computation.19 | convolution fusion | flops 806092416 | bytes 6030848 | tf_op jit(solution)/shard_map/dot_general | solution.py:458
  78.3 0.0 copy-start.1
  78.4 1.1 copy-done.1
  79.5 0.3 multiply_reduce_fusion
  79.8 0.0 copy-done.2
  79.8 8.8 %add_convert_fusion = bf16[384,1024]{1,0:T(8,128)(2,1)} fusion(f32[384,1024]{1,0:T(8,128)} %copy-done.1, bf16[2048,1024]{1,0:T(8,128)(2,1)} %param.21, bf16[1024,2048]{1,0:T(8,128)(2,1)} %param.20, f32[1024]{0:T(1024)S(1)} %bitcast.28, f32[384]{0:T(512)S(1)} %add_rsqrt_fusion, f32[384]{0:T(512)S(1)} %broadcast_multiply_fusion), kind=kOutput, calls=%fused_computation.2 | convolution fusion | flops 3227516928 | bytes 10755072 | tf_op jit(solution)/shard_map/dot_general | solution.py:465
  88.6 25.1 %shard_map.120 = f32[2,128,1024]{2,1,0:T(8,128)} custom-call(s32[2,4]{1,0:T(2,128)} %bitcast.29, bf16[3,128,1024]{2,1,0:T(8,128)(2,1)} %bitcast.24, f32[2,4,128,128]{3,2,1,0:T(8,128)} %bitcast.25), custom_call_target="tpu_custom_call" | custom-call | tf_op jit(solution)/shard_map/pallas_call | solution.py:468
  113.8 2.3 %copy.20 = f32[1,2,128,1024]{3,2,1,0:T(8,128)} copy(f32[1,2,128,1024]{3,2,1,0:T(8,128)} %bitcast.21) | data formatting | bytes 2097152
  (3 shorter events, 0.0 us)
Async XLA Ops:
  0.0 76.1 %copy-start = (bf16[1024,1024]{1,0:T(8,128)(2,1)S(1)}, bf16[1024,1024]{1,0:T(8,128)(2,1)}, u32[]{:S(2)}) copy-start(bf16[1024,1024]{1,0:T(8,128)(2,1)} %param.19) | copy-start | bytes 6291460
  0.0 27.9 %copy-start.3 = (s32[1,3,8]{2,0,1:T(1,128)S(1)}, s32[1,3,8]{2,0,1:T(1,128)}, u32[]{:S(2)}) copy-start(s32[1,3,8]{2,0,1:T(1,128)} %param.15) | copy-start | bytes 292
  28.5 47.6 %copy-start.4 = (f32[3,128,1024]{2,1,0:T(8,128)S(1)}, f32[3,128,1024]{2,1,0:T(8,128)}, u32[]{:S(2)}) copy-start(f32[3,128,1024]{2,1,0:T(8,128)} %get-tuple-element.7) | copy-start | bytes 4718596
  76.1 3.7 %copy-start.2 = (f32[2,1024]{1,0:T(2,128)S(1)}, f32[2,1024]{1,0:T(2,128)}, u32[]{:S(2)}) copy-start(f32[2,1024]{1,0:T(2,128)} %refs_3_.2) | copy-start | bytes 24580
  78.3 1.2 %copy-start.1 = (f32[384,1024]{1,0:T(8,128)}, f32[384,1024]{1,0:T(8,128)S(1)}, u32[]{:S(2)}) copy-start(f32[384,1024]{1,0:T(8,128)S(1)} %get-tuple-element.10) | copy-start | bytes 4718596

commit v3 on v2

--- a/solution.py
+++ b/solution.py
@@ -48,7 +48,8 @@
 
 
 class Halo:
-    def __init__(self, source, table, send_sem, recv_sem, blocks):
+    def __init__(self, source, table, send_sem, recv_sem):
+        blocks = source.shape[0]
         lat_count, lon_count = lax.axis_size("lat"), lax.axis_size("lon")
         lat, lon = lax.axis_index("lat"), lax.axis_index("lon")
         odd = lax.rem(lon, 2)
@@ -227,115 +228,33 @@
     return high, low
 
 
-def lift_kernel(
-    total_lon, blocks, rows,
-    index_ref, grid_ref, weight_ref, gain_ref, mesh_in_ref, normed_ref,
-    table, high_table, low_table, send_sem, recv_sem,
-):
-    halo = Halo(grid_ref, table, send_sem, recv_sem, blocks)
-    halo.greet()
-    halo.start()
-
-    def unpack(source, start, first, many):
-        @pl.loop(0, many)
-        def _(block):
-            high, low = halves(decode(source[start + block]))
-            high_table[first + block] = high
-            low_table[first + block] = low
-
-    unpack(grid_ref, 0, 0, blocks)
-    halo.receive(blocks, lambda first, many: unpack(table, first, first, many))
-
+def interpolate(weight, high_block, low_block):
+    rows = weight.shape[0]
+    high, low = halves(weight)
+    both = jnp.dot(
+        jnp.concatenate([high, low], axis=0), high_block, preferred_element_type=jnp.float32
+    )
+    rest = both[rows:]
+    if low_block is not None:
+        rest = rest + jnp.dot(high, low_block, preferred_element_type=jnp.float32)
+    return both[:rows] + rest
+
+
+def lift(total_lon, blocks, index_ref, weight_ref, gain_ref, high_table, low_table, mesh, normed):
     @pl.loop(0, weight_ref.shape[0])
     def _(target):
         total = None
         for k in range(weight_ref.shape[1]):
             place = find_slot(index_ref[target, k], total_lon, blocks)
-            high, low = halves(weight_ref[target, k])
-            both = jnp.dot(
-                jnp.concatenate([high, low], axis=0),
-                high_table[place],
-                preferred_element_type=jnp.float32,
-            )
-            rest = jnp.dot(high, low_table[place], preferred_element_type=jnp.float32)
-            term = both[:rows] + (both[rows:] + rest)
+            term = interpolate(weight_ref[target, k], high_table[place], low_table[place])
             total = term if total is None else total + term
-        mesh_in_ref[target] = total
-        normed_ref[target] = layer_norm(total, gain_ref[0:1, :])
-
-    halo.finish()
-
-
-def return_kernel(
-    total_lon, blocks, rows,
-    index_ref, mesh_ref, weight_ref, out_ref, table, send_sem, recv_sem,
-):
-    halo = Halo(mesh_ref, table, send_sem, recv_sem, blocks)
-    halo.greet()
-    halo.start()
-    table[pl.ds(0, blocks)] = mesh_ref[...]
-    halo.receive(blocks, lambda first, many: None)
-
-    @pl.loop(0, weight_ref.shape[0])
-    def _(target):
-        total = None
-        for k in range(weight_ref.shape[1]):
-            place = find_slot(index_ref[target, k], total_lon, blocks)
-            high, low = halves(weight_ref[target, k])
-            both = jnp.dot(
-                jnp.concatenate([high, low], axis=0),
-                table[place],
-                preferred_element_type=jnp.float32,
-            )
-            term = both[:rows] + both[rows:]
-            total = term if total is None else total + term
-        out_ref[target] = total
-
-    halo.finish()
-
-
-def attention_kernel(
-    total_lon, blocks, rows, tile,
-    index_ref, count_ref, normed_ref, weight_ref, mixed_ref,
-    table, queries, key_value, send_sem, recv_sem,
-):
-    width = normed_ref.shape[2]
+        mesh[target] = total
+        normed[target] = layer_norm(total, gain_ref[0:1, :])
+
+
+def attention(total_lon, blocks, index_ref, count_ref, queries, key_value, mixed):
+    rows, width = mixed.shape[1:]
     pair = 2 * (width // HEADS)
-    halo = Halo(normed_ref, table, send_sem, recv_sem, blocks)
-    halo.greet()
-    halo.start()
-    scale = (width // HEADS) ** (-0.5)
-
-    @pl.loop(0, width // tile)
-    def _(step):
-        columns = pl.ds(pl.multiple_of(step * tile, tile), tile)
-        product = jnp.dot(
-            normed_ref[...].reshape(blocks * rows, width),
-            weight_ref[:, columns],
-            preferred_element_type=jnp.float32,
-        )
-        product = product.astype(jnp.bfloat16) * jnp.bfloat16(scale)
-        queries[:, :, columns] = product.reshape(blocks, rows, tile)
-
-    def project(source, first, many):
-        @pl.loop(0, 2 * width // tile)
-        def _(step):
-            columns = pl.ds(pl.multiple_of(step * tile, tile), tile)
-            taken = pl.ds(pl.multiple_of(width + step * tile, tile), tile)
-            product = jnp.dot(
-                source[...].reshape(many * rows, width),
-                weight_ref[:, taken],
-                preferred_element_type=jnp.float32,
-            )
-            product = product.astype(jnp.bfloat16).reshape(many, rows, tile)
-            key_value[pl.ds(first, many), :, columns] = product
-
-    def project_slots(first, many):
-        project(table.at[pl.ds(first, many)], first, many)
-
-    project(normed_ref, 0, blocks)
-    halo.receive(blocks, project_slots)
-
     slots = index_ref.shape[1]
     lane = lax.broadcasted_iota(jnp.int32, (rows, pair), 1)
     first_half = lane < pair // 2
@@ -355,18 +274,20 @@
                 [jnp.where(first_half, query, zero), jnp.where(first_half, zero, query)], axis=0
             )
             keys = jnp.concatenate([key_value[place, :, columns] for place in places], axis=0)
-            values = jnp.concatenate([key_value[place, :, value_columns] for place in places], axis=0)
+            values = jnp.concatenate(
+                [key_value[place, :, value_columns] for place in places], axis=0
+            )
             scores = lax.dot_general(
                 both, keys, (((1,), (1,)), ((), ())), preferred_element_type=jnp.float32
             )
             masked = jnp.where(live, scores, -1e30)
             raw = jnp.exp(masked - jnp.max(masked, axis=-1, keepdims=True))
             total = jnp.sum(raw, axis=-1, keepdims=True)
-            mixed = jnp.dot(
+            result = jnp.dot(
                 raw.astype(jnp.bfloat16), values, preferred_element_type=jnp.float32
             ) / total
-            mixed_ref[target, :, columns] = jnp.where(
-                first_half, mixed[:rows], mixed[rows:]
+            mixed[target, :, columns] = jnp.where(
+                first_half, result[:rows], result[rows:]
             ).astype(jnp.bfloat16)
 
         @pl.loop(0, width // pair // 2)
@@ -374,7 +295,128 @@
             attend(2 * step)
             attend(2 * step + 1)
 
-    halo.finish()
+
+def tiled_dot(source, weight, start, end, tile, use):
+    many, rows, depth = source.shape
+
+    @pl.loop(0, (end - start) // tile)
+    def _(step):
+        taken = pl.ds(pl.multiple_of(start + step * tile, tile), tile)
+        given = pl.ds(pl.multiple_of(step * tile, tile), tile)
+        product = jnp.dot(
+            source[...].reshape(many * rows, depth),
+            weight[:, taken],
+            preferred_element_type=jnp.float32,
+        )
+        use(given, product.reshape(many, rows, tile))
+
+
+def layer_kernel(
+    grid_lon, mesh_lon, tile,
+    lift_index, window_index, window_count, return_index, grid_ref, gain_ref,
+    lift_hbm, qkv_hbm, out_hbm, up_hbm, down_hbm, return_hbm,
+    out_ref,
+    lift_weight, qkv_weight, out_weight, up_weight, down_weight, return_weight, load_sem,
+    grid_table, high_table, low_table, normed_table, mesh_table,
+    mesh, normed, queries, key_value, mixed, normed_again, hidden, outgoing,
+    grid_send, grid_recv, normed_send, normed_recv, mesh_send, mesh_recv,
+):
+    grid_blocks = grid_ref.shape[0]
+    blocks, rows, width = mesh.shape
+    loads = [
+        pltpu.make_async_copy(source, target, load_sem.at[number])
+        for number, (source, target) in enumerate(
+            [
+                (lift_hbm, lift_weight),
+                (qkv_hbm, qkv_weight),
+                (out_hbm, out_weight),
+                (up_hbm, up_weight),
+                (down_hbm, down_weight),
+                (return_hbm, return_weight),
+            ]
+        )
+    ]
+    grid_halo = Halo(grid_ref, grid_table, grid_send, grid_recv)
+    normed_halo = Halo(normed, normed_table, normed_send, normed_recv)
+    mesh_halo = Halo(outgoing, mesh_table, mesh_send, mesh_recv)
+
+    grid_halo.greet()
+    grid_halo.start()
+    for load in loads:
+        load.start()
+
+    def unpack(source, start, first, many):
+        @pl.loop(0, many)
+        def _(block):
+            high, low = halves(decode(source[start + block]))
+            high_table[first + block] = high
+            low_table[first + block] = low
+
+    unpack(grid_ref, 0, 0, grid_blocks)
+    grid_halo.receive(grid_blocks, lambda first, many: unpack(grid_table, first, first, many))
+    loads[0].wait()
+    lift(
+        grid_lon, grid_blocks, lift_index, lift_weight, gain_ref, high_table, low_table,
+        mesh, normed,
+    )
+    loads[1].wait()
+
+    normed_halo.start()
+    scale = (width // HEADS) ** (-0.5)
+
+    def keep_queries(columns, product):
+        queries[:, :, columns] = product.astype(jnp.bfloat16) * jnp.bfloat16(scale)
+
+    tiled_dot(normed, qkv_weight, 0, width, tile, keep_queries)
+
+    def project(source, first, many):
+        def keep(columns, product):
+            key_value[pl.ds(first, many), :, columns] = product.astype(jnp.bfloat16)
+
+        tiled_dot(source, qkv_weight, width, 3 * width, tile, keep)
+
+    project(normed, 0, blocks)
+    normed_halo.receive(
+        blocks, lambda first, many: project(normed_table.at[pl.ds(first, many)], first, many)
+    )
+    attention(mesh_lon, blocks, window_index, window_count, queries, key_value, mixed)
+    loads[2].wait()
+    loads[3].wait()
+    loads[4].wait()
+
+    def add_mesh(columns, product):
+        mesh[:, :, columns] = mesh[:, :, columns] + product
+
+    tiled_dot(mixed, out_weight, 0, width, tile, add_mesh)
+    normed_again[...] = layer_norm(mesh[...], gain_ref[1:2, :].reshape(1, 1, width))
+
+    def keep_hidden(columns, product):
+        hidden[:, :, columns] = gelu_exact(product).astype(jnp.bfloat16)
+
+    tiled_dot(normed_again, up_weight, 0, up_weight.shape[1], tile, keep_hidden)
+
+    def keep_outgoing(columns, product):
+        value = (mesh[:, :, columns] + product).astype(jnp.bfloat16)
+        outgoing[:, :, columns] = value
+        mesh_table[pl.ds(0, blocks), :, columns] = value
+
+    tiled_dot(hidden, down_weight, 0, width, tile, keep_outgoing)
+    loads[5].wait()
+    mesh_halo.start()
+    mesh_halo.receive(blocks, lambda first, many: None)
+
+    @pl.loop(0, return_weight.shape[0])
+    def _(target):
+        total = None
+        for k in range(return_weight.shape[1]):
+            place = find_slot(return_index[target, k], mesh_lon, blocks)
+            term = interpolate(return_weight[target, k], mesh_table[place], None)
+            total = term if total is None else total + term
+        out_ref[target] = total
+
+    grid_halo.finish()
+    normed_halo.finish()
+    mesh_halo.finish()
 
 
 def in_vmem(count):
@@ -383,21 +425,6 @@
 
 def in_smem(count):
     return [pl.BlockSpec(memory_space=pltpu.SMEM)] * count
-
-
-def halo_scratch(blocks, rows, width):
-    count = Halo.count(blocks)
-    slots = 3 * (blocks + 2)
-    return (
-        [pltpu.VMEM((slots, rows, width), jnp.bfloat16)],
-        [pltpu.SemaphoreType.DMA((count,)), pltpu.SemaphoreType.DMA((count,))],
-    )
-
-
-def parameters(number):
-    return pltpu.CompilerParams(
-        collective_id=number, has_side_effects=True, vmem_limit_bytes=VMEM_LIMIT
-    )
 
 
 def shards(
@@ -422,60 +449,50 @@
     grid_lon = grid_blocks * lon_count
     mesh_lon = mesh_blocks * lon_count
 
-    grid_table, grid_sems = halo_scratch(grid_blocks, rows, width)
-    mesh_table, mesh_sems = halo_scratch(mesh_blocks, rows, width)
-    mesh_in, normed = pl.pallas_call(
-        lambda *refs: lift_kernel(grid_lon, grid_blocks, rows, *refs),
-        out_shape=(
-            jax.ShapeDtypeStruct((mesh_blocks, rows, width), jnp.float32),
-            jax.ShapeDtypeStruct((mesh_blocks, rows, width), jnp.bfloat16),
+    tile = min(512, width)
+    hidden_width = up_weight.shape[1]
+    half = jnp.bfloat16
+
+    def table(blocks, features, held_as=half):
+        return pltpu.VMEM((blocks, rows, features), held_as)
+
+    grid_slots = 3 * (grid_blocks + 2)
+    mesh_slots = 3 * (mesh_blocks + 2)
+    weights = (lift_weight[0], qkv_weight, out_weight, up_weight, down_weight, return_weight[0])
+    scratch = [pltpu.VMEM(weight.shape, weight.dtype) for weight in weights]
+    scratch += [pltpu.SemaphoreType.DMA((len(weights),))]
+    scratch += [table(grid_slots, width)] * 3 + [table(mesh_slots, width)] * 2
+    scratch += [
+        table(mesh_blocks, width, jnp.float32),
+        table(mesh_blocks, width),
+        table(mesh_blocks, width),
+        table(mesh_slots, 2 * width),
+        table(mesh_blocks, width),
+        table(mesh_blocks, width),
+        table(mesh_blocks, hidden_width),
+        table(mesh_blocks, width),
+    ]
+    for blocks in (grid_blocks, mesh_blocks, mesh_blocks):
+        scratch += [pltpu.SemaphoreType.DMA((Halo.count(blocks),))] * 2
+    grid_out = pl.pallas_call(
+        lambda *refs: layer_kernel(grid_lon, mesh_lon, tile, *refs),
+        out_shape=jax.ShapeDtypeStruct((grid_blocks, rows, width), jnp.float32),
+        in_specs=in_smem(4)
+        + in_vmem(2)
+        + [pl.BlockSpec(memory_space=pl.ANY)] * len(weights),
+        out_specs=in_vmem(1)[0],
+        scratch_shapes=scratch,
+        compiler_params=pltpu.CompilerParams(
+            collective_id=0, has_side_effects=True, vmem_limit_bytes=VMEM_LIMIT
         ),
-        in_specs=in_smem(1) + in_vmem(3),
-        out_specs=tuple(in_vmem(2)),
-        scratch_shapes=grid_table * 3 + grid_sems,
-        compiler_params=parameters(0),
     )(
         lift_index[0],
+        window_index[0],
+        window_count,
+        return_index[0],
         encode(grid_feats[0]),
-        lift_weight[0],
         norm_gains,
-    )
-    tile = min(512, width)
-    mixed = pl.pallas_call(
-        lambda *refs: attention_kernel(mesh_lon, mesh_blocks, rows, tile, *refs),
-        out_shape=jax.ShapeDtypeStruct((mesh_blocks, rows, width), jnp.bfloat16),
-        in_specs=in_smem(2) + in_vmem(2),
-        out_specs=in_vmem(1)[0],
-        scratch_shapes=mesh_table
-        + [
-            pltpu.VMEM((mesh_blocks, rows, width), jnp.bfloat16),
-            pltpu.VMEM((3 * (mesh_blocks + 2), rows, 2 * width), jnp.bfloat16),
-        ]
-        + mesh_sems,
-        compiler_params=parameters(1),
-    )(window_index[0], window_count, normed, qkv_weight)
-    mixed = mixed.reshape(-1, width)
-    after_attention = mesh_in.reshape(-1, width) + jnp.dot(
-        mixed, out_weight, preferred_element_type=jnp.float32
-    )
-    normed_again = layer_norm(after_attention, norm_gains[1])
-    hidden_units = gelu_exact(
-        jnp.dot(normed_again, up_weight, preferred_element_type=jnp.float32)
-    ).astype(jnp.bfloat16)
-    mesh_out = after_attention + jnp.dot(
-        hidden_units, down_weight, preferred_element_type=jnp.float32
-    )
-    grid_out = pl.pallas_call(
-        lambda *refs: return_kernel(mesh_lon, mesh_blocks, rows, *refs),
-        out_shape=jax.ShapeDtypeStruct((grid_blocks, rows, width), jnp.float32),
-        in_specs=in_smem(1) + in_vmem(2),
-        out_specs=in_vmem(1)[0],
-        scratch_shapes=mesh_table + mesh_sems,
-        compiler_params=parameters(2),
-    )(
-        return_index[0],
-        mesh_out.astype(jnp.bfloat16).reshape(mesh_blocks, rows, width),
-        return_weight[0],
+        *weights,
     )
     return grid_out.reshape(1, grid_blocks, rows, width)
 

time: 116 us -> 98.3 us (0.85)
  matrix products: 11 us -> 0 us
  Pallas kernels: 97 us -> 91 us
    dot_general x2 -> x0, matrix products: 11 us -> none  [the longest x1 8.81 us: shards(): jnp.dot(hidden_units, down_weight, preferred_element_type=jnp.float32)]
    pallas_call x3 -> x1, Pallas kernels: 97 us -> 91 us  [shards(): pl.pallas_call(lambda *refs: layer_kernel(grid_lon, mesh_lon, tile, *refs...]
    unnamed x13 -> x3, local copies, waits for them, and re-layouts: 5.33 us -> 4.85 us
where the time goes in v3:
time: 98.3 us; the launch traced here: 98 us
  Pallas kernels  91 us (93%)
  local copies, waits for them, and re-layouts  4.85 us (5%)
  other arithmetic  2.17 us (2%)
    pallas_call x1, Pallas kernels, shards(): pl.pallas_call(lambda *refs: layer_kernel(grid_lon, mesh_lon, tile, *refs...  91 us
    unnamed x3, local copies, waits for them, and re-layouts  4.85 us
    convert_element_type x1, other arithmetic, encode(): return jnp.exp2(values * SPREAD).astype(jnp.bfloat16)  2.17 us

profile of v3, /device:TPU:0, one launch (start us, length us, event | category | flops | bytes accessed | tf_op | source)
XLA Modules:
  0.0 98.0 jit_solution(14102307632460553726)
XLA Ops:
  0.0 1.3 %copy.18 = s32[1,3,4]{2,1,0:T(4,128)} copy(s32[1,3,4]{2,0,1:T(1,128)} %param.13) | data formatting | bytes 96
  1.3 1.3 %copy.17 = s32[1,3,8]{2,1,0:T(4,128)} copy(s32[1,3,8]{2,0,1:T(1,128)} %param.15) | data formatting | bytes 192
  2.5 2.2 %fusion.refs_4_ = bf16[2,128,1024]{2,1,0:T(8,128)(2,1)} fusion(f32[1,2,128,1024]{3,2,1,0:T(8,128)} %param.12), kind=kLoop, calls=%fused_computation.1 | loop fusion | flops 524288 | bytes 1572864 | tf_op jit(solution)/shard_map/convert_element_type | solution.py:218
  4.7 91.0 %shard_map.118 = f32[2,128,1024]{2,1,0:T(8,128)} custom-call(s32[3,4]{1,0:T(4,128)} %bitcast.15, s32[3,8]{1,0:T(4,128)} %bitcast.16, s32[1,3]{1,0:T(1,128)} %refs_2_.1, s32[2,4]{1,0:T(2,128)} %bitcast.17, bf16[2,128,1024]{2,1,0:T(8,128)(2,1)} %fusion.refs_4_, f32[2,1024]{1,0:T(2,128)} %refs_5_.1, f32[3,4,128,128]{3,2,1,0:T(8,128)} %bitcast.13, ...), custom_call_target="tpu_custom_call" | custom-call | tf_op jit(solution)/shard_map/pallas_call | solution.py:477
  95.7 2.3 %copy.20 = f32[1,2,128,1024]{3,2,1,0:T(8,128)} copy(f32[1,2,128,1024]{3,2,1,0:T(8,128)} %bitcast.12) | data formatting | bytes 2097152

commit v4 on v3

--- a/solution.py
+++ b/solution.py
@@ -78,15 +78,22 @@
             copy(source.at[first], table.at[blocks + 1 - odd], self.outer),
             copy(source.at[second], table.at[blocks + odd], self.inner),
         ]
-        ends = [(first, blocks + 2), (second, blocks + 4)]
+        piece = source.shape[1] // 2
+        pieces = [pl.ds(0, piece), pl.ds(piece, piece)]
         self.vertical = []
-        for place, slot in ends:
+        for part in pieces:
             self.vertical.append(
                 (
-                    copy(source.at[place], table.at[slot], self.down),
-                    copy(source.at[place], table.at[slot + 1], self.up),
+                    copy(source.at[first, part], table.at[blocks + 2, part], self.down),
+                    copy(source.at[first, part], table.at[blocks + 3, part], self.up),
                 )
             )
+        self.vertical.append(
+            (
+                copy(source.at[second], table.at[blocks + 4], self.down),
+                copy(source.at[second], table.at[blocks + 5], self.up),
+            )
+        )
         between = blocks + 8
         for place in range(1, blocks - 1):
             slot = between + place - 1
@@ -99,9 +106,11 @@
         last = between + 2 * (blocks - 2)
         self.corners = [
             [
-                copy(table.at[blocks + 2 + band], table.at[last + band], self.outer)
+                copy(table.at[blocks + 2 + band, part], table.at[last + band, part], self.outer)
                 for band in (0, 1)
-            ],
+            ]
+            for part in pieces
+        ] + [
             [
                 copy(table.at[blocks + 4 + band], table.at[blocks + 6 + band], self.inner)
                 for band in (0, 1)
@@ -110,7 +119,7 @@
 
     @staticmethod
     def count(blocks):
-        return 6 + 2 * blocks
+        return 10 + 2 * blocks
 
     def greet(self):
         barrier = pltpu.get_barrier_semaphore()
@@ -172,7 +181,7 @@
             below.wait_recv()
 
     def wait_between(self):
-        for down, up in self.vertical[2:]:
+        for down, up in self.vertical[3:]:
             @pl.when(self.above)
             def _():
                 down.wait_recv()
@@ -182,14 +191,15 @@
                 up.wait_recv()
 
     def receive(self, blocks, work):
-        self.forward(0)
+        self.forward(1)
         self.wait_edges()
         work(blocks, 4)
-        self.forward(1)
-        self.wait_corners(1)
+        self.forward(2)
+        self.wait_corners(2)
         work(blocks + 4, 4)
         self.wait_between()
         self.wait_corners(0)
+        self.wait_corners(1)
         work(blocks + 8, 2 * (blocks - 2) + 2)
 
     def finish(self):
@@ -252,10 +262,10 @@
         normed[target] = layer_norm(total, gain_ref[0:1, :])
 
 
-def attention(total_lon, blocks, index_ref, count_ref, queries, key_value, mixed):
+def attention(total_lon, blocks, skip, index_ref, count_ref, queries, key_value, mixed):
     rows, width = mixed.shape[1:]
     pair = 2 * (width // HEADS)
-    slots = index_ref.shape[1]
+    slots = index_ref.shape[1] - skip
     lane = lax.broadcasted_iota(jnp.int32, (rows, pair), 1)
     first_half = lane < pair // 2
     key_block = lax.broadcasted_iota(jnp.int32, (1, slots * rows), 1) // rows
@@ -263,7 +273,7 @@
     @pl.loop(0, blocks)
     def _(target):
         live = key_block < count_ref[0, target]
-        places = [find_slot(index_ref[target, s], total_lon, blocks) for s in range(slots)]
+        places = [find_slot(index_ref[target, skip + s], total_lon, blocks) for s in range(slots)]
 
         def attend(group):
             columns = pl.ds(pl.multiple_of(group * pair, pair), pair)
@@ -313,7 +323,7 @@
 
 def layer_kernel(
     grid_lon, mesh_lon, tile,
-    lift_index, window_index, window_count, return_index, grid_ref, gain_ref,
+    mesh_index, window_count, return_index, grid_ref, gain_ref,
     lift_hbm, qkv_hbm, out_hbm, up_hbm, down_hbm, return_hbm,
     out_ref,
     lift_weight, qkv_weight, out_weight, up_weight, down_weight, return_weight, load_sem,
@@ -352,11 +362,12 @@
             high_table[first + block] = high
             low_table[first + block] = low
 
+    grid_halo.forward(0)
     unpack(grid_ref, 0, 0, grid_blocks)
     grid_halo.receive(grid_blocks, lambda first, many: unpack(grid_table, first, first, many))
     loads[0].wait()
     lift(
-        grid_lon, grid_blocks, lift_index, lift_weight, gain_ref, high_table, low_table,
+        grid_lon, grid_blocks, mesh_index, lift_weight, gain_ref, high_table, low_table,
         mesh, normed,
     )
     loads[1].wait()
@@ -375,11 +386,12 @@
 
         tiled_dot(source, qkv_weight, width, 3 * width, tile, keep)
 
+    normed_halo.forward(0)
     project(normed, 0, blocks)
     normed_halo.receive(
         blocks, lambda first, many: project(normed_table.at[pl.ds(first, many)], first, many)
     )
-    attention(mesh_lon, blocks, window_index, window_count, queries, key_value, mixed)
+    attention(mesh_lon, blocks, lift_weight.shape[1], mesh_index, window_count, queries, key_value, mixed)
     loads[2].wait()
     loads[3].wait()
     loads[4].wait()
@@ -403,6 +415,7 @@
     tiled_dot(hidden, down_weight, 0, width, tile, keep_outgoing)
     loads[5].wait()
     mesh_halo.start()
+    mesh_halo.forward(0)
     mesh_halo.receive(blocks, lambda first, many: None)
 
     @pl.loop(0, return_weight.shape[0])
@@ -477,7 +490,7 @@
     grid_out = pl.pallas_call(
         lambda *refs: layer_kernel(grid_lon, mesh_lon, tile, *refs),
         out_shape=jax.ShapeDtypeStruct((grid_blocks, rows, width), jnp.float32),
-        in_specs=in_smem(4)
+        in_specs=in_smem(3)
         + in_vmem(2)
         + [pl.BlockSpec(memory_space=pl.ANY)] * len(weights),
         out_specs=in_vmem(1)[0],
@@ -486,8 +499,7 @@
             collective_id=0, has_side_effects=True, vmem_limit_bytes=VMEM_LIMIT
         ),
     )(
-        lift_index[0],
-        window_index[0],
+        jnp.concatenate([lift_index[0], window_index[0]], axis=-1),
         window_count,
         return_index[0],
         encode(grid_feats[0]),

time: 98.3 us -> 99 us (level)
  Pallas kernels: 91 us -> 92.2 us
  local copies, waits for them, and re-layouts: 4.85 us -> 3.67 us
    pallas_call x1, Pallas kernels: 91 us -> 92.2 us  [shards(): pl.pallas_call(lambda *refs: layer_kernel(grid_lon, mesh_lon, tile, *refs...]
    unnamed x3, local copies, waits for them, and re-layouts: 4.85 us -> 3.67 us
where the time goes in v4:
time: 99 us; the launch traced here: 98.7 us
  Pallas kernels  92.2 us (93%)
  local copies, waits for them, and re-layouts  3.67 us (4%)
  other arithmetic  2.83 us (3%)
    pallas_call x1, Pallas kernels, shards(): pl.pallas_call(lambda *refs: layer_kernel(grid_lon, mesh_lon, tile, *refs...  92.2 us
    unnamed x3, local copies, waits for them, and re-layouts  3.67 us
    convert_element_type x1, other arithmetic, encode(): return jnp.exp2(values * SPREAD).astype(jnp.bfloat16)  2.17 us

profile of v4, /device:TPU:0, one launch (start us, length us, event | category | flops | bytes accessed | tf_op | source)
XLA Modules:
  0.0 98.7 jit_solution(8059996476296264631)
XLA Ops:
  0.0 0.7 copy.18
  0.7 0.7 copy.17
  1.4 0.7 pad_add_fusion.refs_0_
  2.0 2.2 %fusion.refs_3_ = bf16[2,128,1024]{2,1,0:T(8,128)(2,1)} fusion(f32[1,2,128,1024]{3,2,1,0:T(8,128)} %param.12), kind=kLoop, calls=%fused_computation.1 | loop fusion | flops 524288 | bytes 1572864 | tf_op jit(solution)/shard_map/convert_element_type | solution.py:228
  4.2 92.2 %shard_map.118 = f32[2,128,1024]{2,1,0:T(8,128)} custom-call(s32[3,12]{1,0:T(4,128)} %pad_add_fusion.refs_0_, s32[1,3]{1,0:T(1,128)} %refs_1_.1, s32[2,4]{1,0:T(2,128)} %bitcast.17, bf16[2,128,1024]{2,1,0:T(8,128)(2,1)} %fusion.refs_3_, f32[2,1024]{1,0:T(2,128)} %refs_4_.1, f32[3,4,128,128]{3,2,1,0:T(8,128)} %bitcast.13, bf16[1024,3072]{1,0:T(8,128)(2,1)} %refs_6_.1, ...), custom_call_target="tpu_custom_call" | custom-call | tf_op jit(solution)/shard_map/pallas_call | solution.py:490
  96.4 2.3 %copy.20 = f32[1,2,128,1024]{3,2,1,0:T(8,128)} copy(f32[1,2,128,1024]{3,2,1,0:T(8,128)} %bitcast.12) | data formatting | bytes 2097152
